TPU v7x, 1024 devices: a whole 4x4x32 slice. The times are simulated.
1024 devices in a mesh: ctx: 128 (over y, z), tp: 8 (over x, core).
Axes of the slice: x: 4, y: 4, z: 32, core: 2. Of those that a mesh axis runs over, the one named last changes fastest.
Arguments:
- tokens: bfloat16 [32768, 2048], P('ctx'), may hold values from -6 to 6
- w_query: bfloat16 [2048, 4096], P(None, 'tp'), may hold values from -0.125 to 0.125
- w_key: bfloat16 [2048, 512], replicated, may hold values from -0.125 to 0.125
- w_value: bfloat16 [2048, 512], replicated, may hold values from -0.125 to 0.125
- w_out: bfloat16 [4096, 2048], P('tp'), may hold values from -0.09375 to 0.09375
- query_gain: float32 [128], replicated, may hold values from 0.5 to 2
- key_gain: float32 [128], replicated, may hold values from 0.5 to 2
- doc_lengths: int32 [256], replicated, may hold values from 1 to 4096, as said below
Outputs:
- layer_out: bfloat16 [32768, 2048], P('ctx', 'tp')
Inputs may be any that keep to these rules, and one draw needn't show every extreme that they name: `doc_lengths`: the lengths sum to 32768; the second-to-last document has exactly 4096 tokens and the last one exactly 128.
All inputs are finite; a program needn't handle non-finite values.
Results may differ from a plain program's by a relative error of at most 0.014.
Values may be sent and summed in bfloat16 or wider, within the bound.
No kernel may reach another device: no remote copies, remote signals or barrier semaphores. Data moves between devices by JAX's collectives and lax.ppermute only.
A program may use at most 32 MiB of HBM per device.

v0:
```python
import functools

import jax
import jax.numpy as jnp
import numpy as np
from jax import lax
from jax.experimental import pallas as pl
from jax.experimental.pallas import tpu as pltpu
from jax.sharding import Mesh, PartitionSpec as P


H = 32
KVH = 4
HD = 128
LINE = 4
EPSILON = 1e-06
ROPE_BASE = 1000000.0
LOG2E = 1.4426950408889634

TP = ("x", "c")
VMEM = pltpu.VMEM
FREQUENCY = ROPE_BASE ** (-2.0 * np.arange(HD // 2, dtype=np.float64) / HD)


def norm_rotate(u, gain, cosine, sine):
    inv = lax.rsqrt(jnp.mean(u * u, axis=-1, keepdims=True) + EPSILON)
    w = u * inv * gain
    return w * cosine + pltpu.roll(w, HD // 2, 1) * sine


def iota(shape, axis):
    return lax.broadcasted_iota(jnp.int32, shape, axis)


def kv_body(
    heads, tokens_hbm, w_key, w_value, gain, lengths, frequency,
    out, cosine, sine, starts, span, tokens, weight, sems,
):
    rows = out.shape[0]
    docs = lengths.shape[1]
    core = lax.axis_index("c")
    block = lax.axis_index("ctx")
    head = (2 * lax.axis_index("x") + core) * heads // (H // KVH)
    columns = pl.ds(pl.multiple_of(head * HD, HD), HD)
    tokens_copy = pltpu.make_async_copy(tokens_hbm, tokens, sems.at[0])
    tokens_copy.start()

    @pl.when(core == 0)
    def _():
        pltpu.make_async_copy(w_key.at[:, columns], weight, sems.at[1]).start()

    @pl.when(core != 0)
    def _():
        pltpu.make_async_copy(w_value.at[:, columns], weight, sems.at[1]).start()

    counts = lengths[...].astype(jnp.float32)
    before = iota((docs, docs), 1) <= iota((docs, docs), 0)
    ends = jnp.sum(jnp.where(before, counts, 0.0), axis=1, keepdims=True)
    here = (block * rows + iota((docs, rows), 1)).astype(jnp.float32)
    start_row = jnp.max(jnp.where(ends <= here, ends, 0.0), axis=0, keepdims=True)
    same = iota((rows, rows), 0) == iota((rows, rows), 1)
    start_column = jnp.sum(jnp.where(same, start_row, 0.0), axis=1, keepdims=True)
    starts[...] = start_column.astype(jnp.int32)
    span[0] = jnp.min(start_row).astype(jnp.int32)
    span[1] = jnp.max(start_row).astype(jnp.int32)
    offsets = (block * rows + iota((rows, 1), 0)).astype(jnp.float32) - start_column
    angles = offsets * frequency[...]
    cosine[...] = jnp.cos(angles)
    lower = iota((rows, HD), 1) < HD // 2
    turned = jnp.sin(angles)
    sine[...] = jnp.where(lower, -turned, turned)

    tokens_copy.wait()
    pltpu.make_async_copy(w_key.at[:, columns], weight, sems.at[1]).wait()
    u = jnp.dot(tokens[...], weight[...], preferred_element_type=jnp.float32)

    @pl.when(core == 0)
    def _():
        out[...] = norm_rotate(u, gain[...], cosine[...], sine[...]).astype(out.dtype)

    @pl.when(core != 0)
    def _():
        out[...] = u.astype(out.dtype)


def project_kv(tokens, w_key, w_value, gain, lengths, heads):
    rows, width = tokens.shape
    frequency = jnp.asarray(np.tile(FREQUENCY, 2)[None], jnp.float32)
    table = jax.ShapeDtypeStruct((rows, HD), jnp.float32)
    return pl.pallas_call(
        functools.partial(kv_body, heads),
        out_shape=(
            jax.ShapeDtypeStruct((rows, HD), jnp.bfloat16),
            table,
            table,
            jax.ShapeDtypeStruct((rows, 1), jnp.int32),
            jax.ShapeDtypeStruct((2,), jnp.int32),
        ),
        in_specs=[pl.BlockSpec(memory_space=pltpu.HBM)] * 3
        + [pl.BlockSpec(memory_space=VMEM)] * 3,
        out_specs=(pl.BlockSpec(memory_space=VMEM),) * 4
        + (pl.BlockSpec(memory_space=pltpu.SMEM),),
        scratch_shapes=[
            VMEM((rows, width), tokens.dtype),
            VMEM((width, HD), w_key.dtype),
            pltpu.SemaphoreType.DMA((2,)),
        ],
        cost_estimate=pl.CostEstimate(
            flops=2 * rows * width * HD, bytes_accessed=4 * rows * width, transcendentals=0
        ),
        compiler_params=pltpu.CompilerParams(vmem_limit_bytes=63 << 20),
        name="project_kv",
    )(tokens, w_key, w_value, gain, lengths, frequency)


def q_body(heads, tokens, w_query, gain, cosine, sine, out):
    u = jnp.dot(tokens[...], w_query[...], preferred_element_type=jnp.float32)
    for h in range(heads):
        part = u[:, h * HD : (h + 1) * HD]
        out[h] = norm_rotate(part, gain[...], cosine[...], sine[...]).astype(out.dtype)


def project_q(tokens, w_query, gain, cosine, sine):
    rows, width = tokens.shape
    heads = w_query.shape[1] // HD
    return pl.pallas_call(
        functools.partial(q_body, heads),
        out_shape=jax.ShapeDtypeStruct((heads, rows, HD), jnp.bfloat16),
        in_specs=[pl.BlockSpec(memory_space=VMEM)] * 5,
        out_specs=pl.BlockSpec(memory_space=VMEM),
        cost_estimate=pl.CostEstimate(
            flops=2 * rows * width * heads * HD, bytes_accessed=6 * rows * width, transcendentals=0
        ),
        compiler_params=pltpu.CompilerParams(vmem_limit_bytes=10 << 20),
        name="project_q",
    )(tokens, w_query, gain, cosine, sine)


def add_block(heads, queries, key, value, total, weighted, mask):
    for h in range(heads):
        scores = lax.dot_general(
            queries[h], key, (((1,), (1,)), ((), ())), preferred_element_type=jnp.float32
        )
        weights = jnp.exp2(scores * (HD**-0.5 * LOG2E))
        if mask is not None:
            weights = weights * mask[...]
        total[h] += weights[:, :HD] + weights[:, HD:]
        weighted[h] += jnp.dot(
            weights.astype(jnp.bfloat16), value, preferred_element_type=jnp.float32
        )


def add_blocks(heads, distance_of, places, span, queries, starts, kv, total, weighted, mask):
    rows = queries.shape[1]
    block = lax.axis_index("ctx")
    first = span[0] // rows
    last = span[1]

    def step(place, carry):
        b = block - distance_of(place)

        @pl.when(b >= first)
        def _():
            key, value = kv[0, place], kv[1, place]
            whole = (b < block) & (b * rows >= last)

            @pl.when(whole)
            def _():
                add_block(heads, queries, key, value, total, weighted, None)

            @pl.when(jnp.logical_not(whole))
            def _():
                key_pos = b * rows + iota((rows, rows), 1)
                query_pos = block * rows + iota((rows, rows), 0)
                visible = (key_pos <= query_pos) & (key_pos >= starts[...])
                mask[...] = jnp.where(visible, 1.0, 0.0)
                add_block(heads, queries, key, value, total, weighted, mask)

        return carry

    lax.fori_loop(0, places, step, 0)


def start_copies(mine, theirs, kv, sems):
    core = lax.axis_index("c")
    copies = []
    for side, group in ((core, mine), (1 - core, theirs)):
        at = 0
        for ref in group:
            count = ref.shape[0]
            copies.append(
                pltpu.make_async_copy(
                    ref, kv.at[side, pl.ds(at, count)], sems.at[len(copies)]
                )
            )
            at += count
    for copy in copies:
        copy.start()
    return copies


def near_body(heads, n, span, queries, starts, *refs):
    mine, theirs = refs[:n], refs[n : 2 * n]
    total, weighted, mask, kv, sems = refs[2 * n :]
    copies = start_copies(mine, theirs, kv, sems)
    total[...] = jnp.zeros_like(total)
    weighted[...] = jnp.zeros_like(weighted)
    for copy in copies:
        copy.wait()

    def distance_of(place):
        return jnp.where(
            place == 0, 0, 1 + (place - 1) // LINE + LINE * ((place - 1 + LINE) % LINE)
        )

    add_blocks(
        heads, distance_of, kv.shape[1], span, queries, starts, kv, total, weighted, mask
    )


def attend_near(span, queries, starts, mine, theirs):
    heads, rows, _ = queries.shape
    n = len(mine)
    places = sum(a.shape[0] for a in mine)
    state = jax.ShapeDtypeStruct((heads, rows, HD), jnp.float32)
    return pl.pallas_call(
        functools.partial(near_body, heads, n),
        out_shape=(state, state),
        in_specs=[pl.BlockSpec(memory_space=pltpu.SMEM)]
        + [pl.BlockSpec(memory_space=VMEM)] * 2
        + [pl.BlockSpec(memory_space=pl.ANY)] * (2 * n),
        out_specs=(pl.BlockSpec(memory_space=VMEM),) * 2,
        scratch_shapes=[
            VMEM((rows, rows), jnp.float32),
            VMEM((2, places, rows, HD), jnp.bfloat16),
            pltpu.SemaphoreType.DMA((2 * n,)),
        ],
        cost_estimate=pl.CostEstimate(
            flops=16 * places * heads * rows * rows * HD, bytes_accessed=2 << 20, transcendentals=0
        ),
        compiler_params=pltpu.CompilerParams(vmem_limit_bytes=12 << 20),
        name="attend_near",
    )(span, queries, starts, *mine, *theirs)


def far_body(heads, n, span, queries, starts, total_in, weighted_in, *refs):
    mine, theirs = refs[:n], refs[n : 2 * n]
    w_out_any, keep, give, total, weighted, mask, attended, kv, w_out, sems = refs[2 * n :]
    copies = start_copies(mine, theirs, kv, sems)
    weights_copy = pltpu.make_async_copy(w_out_any, w_out, sems.at[2 * n])
    weights_copy.start()
    core = lax.axis_index("c")
    total[...] = total_in[...]
    weighted[...] = weighted_in[...]
    for copy in copies:
        copy.wait()

    def distance_of(place):
        return LINE - n + 1 + place // LINE + LINE * (place % LINE)

    add_blocks(
        heads, distance_of, kv.shape[1], span, queries, starts, kv, total, weighted, mask
    )
    for h in range(heads):
        sums = jnp.sum(total[h], axis=1, keepdims=True)
        attended[:, h * HD : (h + 1) * HD] = (weighted[h] / sums).astype(attended.dtype)
    weights_copy.wait()
    width = keep.shape[2]
    for out, side in ((give, 1 - core), (keep, core)):
        for x in range(keep.shape[0]):
            columns = pl.ds(pl.multiple_of((2 * x + side) * width, width), width)
            out[x] = jnp.dot(
                attended[...], w_out[:, columns], preferred_element_type=jnp.float32
            ).astype(out.dtype)


def attend_far(span, queries, starts, total, weighted, mine, theirs, w_out, chips):
    heads, rows, _ = queries.shape
    n = len(mine)
    places = sum(a.shape[0] for a in mine)
    width = w_out.shape[1] // (2 * chips)
    half = jax.ShapeDtypeStruct((chips, rows, width), jnp.bfloat16)
    return pl.pallas_call(
        functools.partial(far_body, heads, n),
        out_shape=(half, half),
        in_specs=[pl.BlockSpec(memory_space=pltpu.SMEM)]
        + [pl.BlockSpec(memory_space=VMEM)] * 4
        + [pl.BlockSpec(memory_space=pl.ANY)] * (2 * n + 1),
        out_specs=(pl.BlockSpec(memory_space=VMEM),) * 2,
        scratch_shapes=[
            VMEM((heads, rows, HD), jnp.float32),
            VMEM((heads, rows, HD), jnp.float32),
            VMEM((rows, rows), jnp.float32),
            VMEM((rows, heads * HD), jnp.bfloat16),
            VMEM((2, places, rows, HD), jnp.bfloat16),
            VMEM(w_out.shape, jnp.bfloat16),
            pltpu.SemaphoreType.DMA((2 * n + 1,)),
        ],
        cost_estimate=pl.CostEstimate(
            flops=4 * places * heads * rows * rows * HD, bytes_accessed=4 << 20, transcendentals=0
        ),
        compiler_params=pltpu.CompilerParams(vmem_limit_bytes=16 << 20),
        name="attend_far",
    )(span, queries, starts, total, weighted, *mine, *theirs, w_out)


def passed_along(a, distance):
    n = lax.axis_size("ctx")
    return lax.ppermute(a, "ctx", [(i, i + distance) for i in range(n - distance)])


def swapped(a):
    return lax.ppermute(a, "c", [(0, 1), (1, 0)])


def local(tokens, w_query, w_key, w_value, w_out, query_gain, key_gain, doc_lengths):
    heads = w_query.shape[1] // HD
    chips = lax.axis_size("x")
    part, cosine, sine, starts, span = project_kv(
        tokens, w_key, w_value, key_gain[None], doc_lengths[None], heads
    )
    own = part[None]
    far = [passed_along(part, LINE + 1)]
    far.append(passed_along(far[-1], LINE))
    queries = project_q(tokens, w_query, query_gain[None], cosine, sine)
    middle, queries = lax.optimization_barrier((far[-1], queries))
    far.append(passed_along(middle, LINE))
    hops = [jnp.stack([passed_along(part, 1)] + far)]
    theirs = [swapped(own)]
    for _ in range(LINE - 1):
        hop, theirs = lax.optimization_barrier((hops[-1], theirs))
        hops.append(passed_along(hop, 1))
        theirs = theirs + [swapped(hop)]
    mine = [own] + hops

    state = attend_near(span, queries, starts, mine[:3], theirs[:3])
    last, (total, weighted) = lax.optimization_barrier((hops[-1], state))
    theirs.append(swapped(last))
    keep, give = attend_far(
        span, queries, starts, total, weighted, mine[3:], theirs[3:], w_out, chips
    )
    pairs = (keep.astype(jnp.float32) + swapped(give).astype(jnp.float32)).astype(jnp.bfloat16)
    terms = lax.all_to_all(pairs, "x", 0, 0, tiled=True)
    return jnp.sum(terms.astype(jnp.float32), axis=0).astype(jnp.bfloat16)


def solution(mesh):
    ctx, tp = mesh.shape["ctx"], mesh.shape["tp"]
    fine = Mesh(mesh.devices.reshape(ctx, tp // 2, 2), ("ctx",) + TP)
    return jax.shard_map(
        local,
        mesh=fine,
        in_specs=(P("ctx", None), P(None, TP), P(), P(), P(TP, None), P(), P(), P()),
        out_specs=P("ctx", TP),
        check_vma=False,
    )
```

profile of v0, /device:TPU:24, one launch (start us, length us, event | category | flops | bytes accessed | tf_op | source)
XLA Modules:
  0.0 127.2 jit_solution(12717412426501747752)
XLA Ops:
  0.0 0.0 copy-start.7
  0.0 4.1 %project_kv.1 = (bf16[256,128]{1,0:T(8,128)(2,1)}, f32[256,128]{1,0:T(8,128)}, f32[256,128]{1,0:T(8,128)}, s32[256,1]{1,0:T(8,128)}, s32[2]{0:T(128)}) custom-call(bf16[256,2048]{1,0:T(8,128)(2,1)} %tokens.1, bf16[2048,512]{1,0:T(8,128)(2,1)} %w_key.1, bf16[2048,512]{1,0:T(8,128)(2,1)} %w_value.1, f32[1,128]{1,0:T(1,128)} %bitcast.16, s32[1,256]{1,0:T(1,128)} %bitcast.15, ...), custom_call_target="tpu_custom_call" | custom-call | flops 134217728 | bytes 2097152 | tf_op jit(solution)/shard_map/project_kv/pallas_call | solution.py:90
  4.1 10.5 %collective-permute-start = (bf16[256,128]{1,0:T(8,128)(2,1)}, bf16[256,128]{1,0:T(8,128)(2,1)S(1)}, u32[]{:S(2)}, u32[]{:S(2)}) collective-permute-start(bf16[256,128]{1,0:T(8,128)(2,1)} %get-tuple-element.29), channel_id=1, source_target_pairs={{0,40},{8,48},{16,56},{24,64},{32,72},{40,80},{48,88},{56,96},{64,... | collective-permute-start | bytes 196616 | tf_op jit(solution)/shard_map/ppermute | solution.py:309
  14.5 13.9 %collective-permute-done = bf16[256,128]{1,0:T(8,128)(2,1)S(1)} collective-permute-done((bf16[256,128]{1,0:T(8,128)(2,1)}, bf16[256,128]{1,0:T(8,128)(2,1)S(1)}, u32[]{:S(2)}, u32[]{:S(2)}) %collective-permute-start) | collective-permute-done | bytes 65568 | tf_op jit(solution)/shard_map/ppermute | solution.py:309
  28.5 9.5 %collective-permute-start.1 = (bf16[256,128]{1,0:T(8,128)(2,1)S(1)}, bf16[256,128]{1,0:T(8,128)(2,1)S(1)}, u32[]{:S(2)}, u32[]{:S(2)}) collective-permute-start(bf16[256,128]{1,0:T(8,128)(2,1)S(1)} %collective-permute-done), channel_id=1, source_target_pairs={{0,32},{8,40},{16,48},{24,56},{32,64},{40,72},{48,80},{56,88},{64,... | collective-permute-start | bytes 196616 | tf_op jit(solution)/shard_map/ppermute | solution.py:309
  37.9 1.9 %collective-permute-start.2 = (bf16[256,128]{1,0:T(8,128)(2,1)}, bf16[256,128]{1,0:T(8,128)(2,1)S(1)}, u32[]{:S(2)}, u32[]{:S(2)}) collective-permute-start(bf16[256,128]{1,0:T(8,128)(2,1)} %get-tuple-element.29), channel_id=1, source_target_pairs={{0,8},{8,16},{16,24},{24,32},{32,40},{40,48},{48,56},{56,64},{64,7... | collective-permute-start | bytes 196616 | tf_op jit(solution)/shard_map/ppermute | solution.py:309
  39.9 0.0 copy-done.7
  39.9 0.0 copy-start
  39.9 1.2 copy-done
  41.1 0.0 copy-start.2
  41.1 1.6 %copy-done.2 = bf16[2048,512]{1,0:T(8,128)(2,1)S(1)} copy-done((bf16[2048,512]{1,0:T(8,128)(2,1)S(1)}, bf16[2048,512]{1,0:T(8,128)(2,1)}, u32[]{:S(2)}) %copy-start.2) | copy-done | bytes 2097176
  42.7 0.0 copy-start.4
  42.7 0.9 copy-done.4
  43.6 0.0 copy-start.5
  43.6 0.9 copy-done.5
  44.5 0.0 copy-start.8
  44.5 0.0 copy-start.3
  44.5 0.0 copy-start.6
  44.5 1.0 project_q.1.queries
  45.5 0.0 collective-permute-done.1
  45.5 2.5 %collective-permute-start.3 = (bf16[256,128]{1,0:T(8,128)(2,1)S(1)}, bf16[256,128]{1,0:T(8,128)(2,1)S(1)}, u32[]{:S(2)}, u32[]{:S(2)}) collective-permute-start(bf16[256,128]{1,0:T(8,128)(2,1)S(1)} %collective-permute-done.1), channel_id=1, source_target_pairs={{0,32},{8,40},{16,48},{24,56},{32,64},{40,72},{48,80},{56,88},{64,... | collective-permute-start | bytes 196616 | tf_op jit(solution)/shard_map/ppermute | solution.py:309
  48.0 0.0 copy-done.8
  48.0 1.9 %collective-permute-start.4 = (bf16[1,256,128]{2,1,0:T(8,128)(2,1)S(1)}, bf16[1,256,128]{2,1,0:T(8,128)(2,1)S(1)}, u32[]{:S(2)}, u32[]{:S(2)}) collective-permute-start(bf16[1,256,128]{2,1,0:T(8,128)(2,1)S(1)} %bitcast.9), channel_id=1, source_target_pairs={{0,1},{1,0},{2,3},{3,2},{4,5},{5,4},{6,7},{7,6},{8,9},{9,8},{10,11... | collective-permute-start | bytes 196616 | tf_op jit(solution)/shard_map/ppermute | solution.py:313
  49.9 0.0 collective-permute-done.2
  50.0 6.5 %collective-permute-done.3 = bf16[256,128]{1,0:T(8,128)(2,1)S(1)} collective-permute-done((bf16[256,128]{1,0:T(8,128)(2,1)S(1)}, bf16[256,128]{1,0:T(8,128)(2,1)S(1)}, u32[]{:S(2)}, u32[]{:S(2)}) %collective-permute-start.3) | collective-permute-done | bytes 65568 | tf_op jit(solution)/shard_map/ppermute | solution.py:309
  56.5 0.0 collective-permute-done.4.refs_3_
  56.5 1.9 %collective-permute-start.6 = (bf16[4,256,128]{2,1,0:T(8,128)(2,1)S(1)}, bf16[4,256,128]{2,1,0:T(8,128)(2,1)S(1)}, u32[]{:S(2)}, u32[]{:S(2)}) collective-permute-start(bf16[4,256,128]{2,1,0:T(8,128)(2,1)S(1)} %pad_maximum_fusion.refs_1_), channel_id=1, source_target_pairs={{0,1},{1,0},{2,3},{3,2},{4,5},{5,4},{6,7},{7,6},{8,9},{9,8},{10,11... | collective-permute-start | bytes 786440 | tf_op jit(solution)/shard_map/ppermute | solution.py:313
  58.5 1.9 %collective-permute-start.5 = (bf16[4,256,128]{2,1,0:T(8,128)(2,1)S(1)}, bf16[4,256,128]{2,1,0:T(8,128)(2,1)S(1)}, u32[]{:S(2)}, u32[]{:S(2)}) collective-permute-start(bf16[4,256,128]{2,1,0:T(8,128)(2,1)S(1)} %pad_maximum_fusion.refs_1_), channel_id=1, source_target_pairs={{0,8},{8,16},{16,24},{24,32},{32,40},{40,48},{48,56},{56,64},{64,7... | collective-permute-start | bytes 786440 | tf_op jit(solution)/shard_map/ppermute | solution.py:309
  60.4 0.0 collective-permute-done.6.refs_4_
  60.4 10.8 %collective-permute-done.5.refs_2_ = bf16[4,256,128]{2,1,0:T(8,128)(2,1)S(1)} collective-permute-done((bf16[4,256,128]{2,1,0:T(8,128)(2,1)S(1)}, bf16[4,256,128]{2,1,0:T(8,128)(2,1)S(1)}, u32[]{:S(2)}, u32[]{:S(2)}) %collective-permute-start.5) | collective-permute-done | bytes 262176 | tf_op jit(solution)/shard_map/ppermute | solution.py:309
  71.2 1.9 %collective-permute-start.8 = (bf16[4,256,128]{2,1,0:T(8,128)(2,1)S(1)}, bf16[4,256,128]{2,1,0:T(8,128)(2,1)S(1)}, u32[]{:S(2)}, u32[]{:S(2)}) collective-permute-start(bf16[4,256,128]{2,1,0:T(8,128)(2,1)S(1)} %collective-permute-done.5.refs_2_), channel_id=1, source_target_pairs={{0,1},{1,0},{2,3},{3,2},{4,5},{5,4},{6,7},{7,6},{8,9},{9,8},{10,11... | collective-permute-start | bytes 786440 | tf_op jit(solution)/shard_map/ppermute | solution.py:313
  73.1 1.9 %collective-permute-start.7 = (bf16[4,256,128]{2,1,0:T(8,128)(2,1)S(1)}, bf16[4,256,128]{2,1,0:T(8,128)(2,1)S(1)}, u32[]{:S(2)}, u32[]{:S(2)}) collective-permute-start(bf16[4,256,128]{2,1,0:T(8,128)(2,1)S(1)} %collective-permute-done.5.refs_2_), channel_id=1, source_target_pairs={{0,8},{8,16},{16,24},{24,32},{32,40},{40,48},{48,56},{56,64},{64,7... | collective-permute-start | bytes 786440 | tf_op jit(solution)/shard_map/ppermute | solution.py:309
  75.0 0.0 collective-permute-done.8.refs_5_
  75.0 10.8 %collective-permute-done.7.refs_0_ = bf16[4,256,128]{2,1,0:T(8,128)(2,1)S(1)} collective-permute-done((bf16[4,256,128]{2,1,0:T(8,128)(2,1)S(1)}, bf16[4,256,128]{2,1,0:T(8,128)(2,1)S(1)}, u32[]{:S(2)}, u32[]{:S(2)}) %collective-permute-start.7) | collective-permute-done | bytes 262176 | tf_op jit(solution)/shard_map/ppermute | solution.py:309
  85.8 1.9 %collective-permute-start.10 = (bf16[4,256,128]{2,1,0:T(8,128)(2,1)S(1)}, bf16[4,256,128]{2,1,0:T(8,128)(2,1)S(1)}, u32[]{:S(2)}, u32[]{:S(2)}) collective-permute-start(bf16[4,256,128]{2,1,0:T(8,128)(2,1)S(1)} %collective-permute-done.7.refs_0_), channel_id=1, source_target_pairs={{0,1},{1,0},{2,3},{3,2},{4,5},{5,4},{6,7},{7,6},{8,9},{9,8},{10,11... | collective-permute-start | bytes 786440 | tf_op jit(solution)/shard_map/ppermute | solution.py:313
  87.7 1.9 %collective-permute-start.9 = (bf16[4,256,128]{2,1,0:T(8,128)(2,1)S(1)}, bf16[4,256,128]{2,1,0:T(8,128)(2,1)S(1)}, u32[]{:S(2)}, u32[]{:S(2)}) collective-permute-start(bf16[4,256,128]{2,1,0:T(8,128)(2,1)S(1)} %collective-permute-done.7.refs_0_), channel_id=1, source_target_pairs={{0,8},{8,16},{16,24},{24,32},{32,40},{40,48},{48,56},{56,64},{64,7... | collective-permute-start | bytes 786440 | tf_op jit(solution)/shard_map/ppermute | solution.py:309
  89.7 0.0 copy-done.3
  89.7 0.0 copy-done.6
  89.7 0.0 copy-start.1
  89.7 6.0 %attend_near.1 = (f32[4,256,128]{2,1,0:T(8,128)S(1)}, f32[4,256,128]{2,1,0:T(8,128)S(1)}) custom-call(s32[2]{0:T(128)S(1)} %copy-done.6, bf16[4,256,128]{2,1,0:T(8,128)(2,1)S(1)} %project_q.1.queries, s32[256,1]{1,0:T(8,128)S(1)} %copy-done.3, bf16[1,256,128]{2,1,0:T(8,128)(2,1)S(1)} %bitcast.10, bf16[4,256,128]{2,1,0:T(8,128)(2,1)S(1)} %pad_maximum_fusion.refs_1_, ...), custom_call_target="tpu_custom_call" | custom-call | flops 4831838208 | bytes 2097152 | tf_op jit(solution)/shard_map/attend_near/pallas_call | solution.py:226
  95.7 4.7 %collective-permute-done.9.refs_1_ = bf16[4,256,128]{2,1,0:T(8,128)(2,1)S(1)} collective-permute-done((bf16[4,256,128]{2,1,0:T(8,128)(2,1)S(1)}, bf16[4,256,128]{2,1,0:T(8,128)(2,1)S(1)}, u32[]{:S(2)}, u32[]{:S(2)}) %collective-permute-start.9) | collective-permute-done | bytes 262176 | tf_op jit(solution)/shard_map/ppermute | solution.py:309
  100.4 1.9 %collective-permute-start.11 = (bf16[4,256,128]{2,1,0:T(8,128)(2,1)S(1)}, bf16[4,256,128]{2,1,0:T(8,128)(2,1)S(1)}, u32[]{:S(2)}, u32[]{:S(2)}) collective-permute-start(bf16[4,256,128]{2,1,0:T(8,128)(2,1)S(1)} %collective-permute-done.9.refs_1_), channel_id=1, source_target_pairs={{0,1},{1,0},{2,3},{3,2},{4,5},{5,4},{6,7},{7,6},{8,9},{9,8},{10,11... | collective-permute-start | bytes 786440 | tf_op jit(solution)/shard_map/ppermute | solution.py:313
  102.4 0.0 collective-permute-done.10.refs_2_
  102.4 1.5 %collective-permute-done.11.refs_3_ = bf16[4,256,128]{2,1,0:T(8,128)(2,1)S(1)} collective-permute-done((bf16[4,256,128]{2,1,0:T(8,128)(2,1)S(1)}, bf16[4,256,128]{2,1,0:T(8,128)(2,1)S(1)}, u32[]{:S(2)}, u32[]{:S(2)}) %collective-permute-start.11) | collective-permute-done | bytes 262176 | tf_op jit(solution)/shard_map/ppermute | solution.py:313
  103.9 0.0 copy-done.1
  103.9 4.8 %attend_far.1 = (bf16[4,256,256]{2,1,0:T(8,128)(2,1)S(1)}, bf16[4,256,256]{2,1,0:T(8,128)(2,1)S(1)}) custom-call(s32[2]{0:T(128)S(1)} %copy-done.6, bf16[4,256,128]{2,1,0:T(8,128)(2,1)S(1)} %project_q.1.queries, s32[256,1]{1,0:T(8,128)S(1)} %copy-done.3, f32[4,256,128]{2,1,0:T(8,128)S(1)} %get-tuple-element.46.total_in, ...), custom_call_target="tpu_custom_call" | custom-call | flops 1073741824 | bytes 4194304 | tf_op jit(solution)/shard_map/attend_far/pallas_call | solution.py:283
  108.6 2.1 %collective-permute-start.12 = (bf16[4,256,256]{2,1,0:T(8,128)(2,1)S(1)}, bf16[4,256,256]{2,1,0:T(8,128)(2,1)S(1)}, u32[]{:S(2)}, u32[]{:S(2)}) collective-permute-start(bf16[4,256,256]{2,1,0:T(8,128)(2,1)S(1)} %get-tuple-element.50), channel_id=1, source_target_pairs={{0,1},{1,0},{2,3},{3,2},{4,5},{5,4},{6,7},{7,6},{8,9},{9,8},{10,11... | collective-permute-start | bytes 1572872 | tf_op jit(solution)/shard_map/ppermute | solution.py:313
  110.7 1.7 %collective-permute-done.12 = bf16[4,256,256]{2,1,0:T(8,128)(2,1)S(1)} collective-permute-done((bf16[4,256,256]{2,1,0:T(8,128)(2,1)S(1)}, bf16[4,256,256]{2,1,0:T(8,128)(2,1)S(1)}, u32[]{:S(2)}, u32[]{:S(2)}) %collective-permute-start.12) | collective-permute-done | bytes 524320 | tf_op jit(solution)/shard_map/ppermute | solution.py:313
  112.4 0.1 add_convert_fusion
  112.6 13.9 %all_to_all.5 = bf16[4,256,256]{2,1,0:T(8,128)(2,1)S(1)} all-to-all(bf16[4,256,256]{2,1,0:T(8,128)(2,1)S(1)} %add_convert_fusion), channel_id=1, replica_groups=mesh['ctx'=128,'x'=4,'c'=2] {'x'}, dimensions={0} | all-to-all | bytes 1048576 | tf_op jit(solution)/shard_map/all_to_all | solution.py:343
  126.5 0.7 reduce_sum.12
  (1 shorter events, 0.0 us)
Async XLA Ops:
  0.0 39.9 %copy-start.7 = (f32[128]{0:T(128)S(1)}, f32[128]{0:T(128)}, u32[]{:S(2)}) copy-start(f32[128]{0:T(128)} %param.14) | copy-start | bytes 1540
  4.1 24.4 %collective-permute-start = (bf16[256,128]{1,0:T(8,128)(2,1)}, bf16[256,128]{1,0:T(8,128)(2,1)S(1)}, u32[]{:S(2)}, u32[]{:S(2)}) collective-permute-start(bf16[256,128]{1,0:T(8,128)(2,1)} %get-tuple-element.29), channel_id=1, source_target_pairs={{0,40},{8,48},{16,56},{24,64},{32,72},{40,80},{48,88},{56,96},{64,... | collective-permute-start | bytes 196616 | tf_op jit(solution)/shard_map/ppermute | solution.py:309
  28.5 17.0 %collective-permute-start.1 = (bf16[256,128]{1,0:T(8,128)(2,1)S(1)}, bf16[256,128]{1,0:T(8,128)(2,1)S(1)}, u32[]{:S(2)}, u32[]{:S(2)}) collective-permute-start(bf16[256,128]{1,0:T(8,128)(2,1)S(1)} %collective-permute-done), channel_id=1, source_target_pairs={{0,32},{8,40},{16,48},{24,56},{32,64},{40,72},{48,80},{56,88},{64,... | collective-permute-start | bytes 196616 | tf_op jit(solution)/shard_map/ppermute | solution.py:309
  37.9 12.0 %collective-permute-start.2 = (bf16[256,128]{1,0:T(8,128)(2,1)}, bf16[256,128]{1,0:T(8,128)(2,1)S(1)}, u32[]{:S(2)}, u32[]{:S(2)}) collective-permute-start(bf16[256,128]{1,0:T(8,128)(2,1)} %get-tuple-element.29), channel_id=1, source_target_pairs={{0,8},{8,16},{16,24},{24,32},{32,40},{40,48},{48,56},{56,64},{64,7... | collective-permute-start | bytes 196616 | tf_op jit(solution)/shard_map/ppermute | solution.py:309
  39.9 1.2 copy-start
  41.1 1.6 %copy-start.2 = (bf16[2048,512]{1,0:T(8,128)(2,1)S(1)}, bf16[2048,512]{1,0:T(8,128)(2,1)}, u32[]{:S(2)}) copy-start(bf16[2048,512]{1,0:T(8,128)(2,1)} %w_query.1) | copy-start | bytes 6291460
  42.7 0.9 copy-start.4
  43.6 0.9 copy-start.5
  44.5 3.5 %copy-start.8 = (bf16[256,128]{1,0:T(8,128)(2,1)S(1)}, bf16[256,128]{1,0:T(8,128)(2,1)}, u32[]{:S(2)}) copy-start(bf16[256,128]{1,0:T(8,128)(2,1)} %get-tuple-element.29) | copy-start | bytes 196612
  44.5 45.2 %copy-start.3 = (s32[256,1]{1,0:T(8,128)S(1)}, s32[256,1]{1,0:T(8,128)}, u32[]{:S(2)}) copy-start(s32[256,1]{1,0:T(8,128)} %get-tuple-element.33.starts) | copy-start | bytes 3076
  44.5 45.2 %copy-start.6 = (s32[2]{0:T(128)S(1)}, s32[2]{0:T(128)}, u32[]{:S(2)}) copy-start(s32[2]{0:T(128)} %get-tuple-element.28.span) | copy-start | bytes 28
  45.5 11.0 %collective-permute-start.3 = (bf16[256,128]{1,0:T(8,128)(2,1)S(1)}, bf16[256,128]{1,0:T(8,128)(2,1)S(1)}, u32[]{:S(2)}, u32[]{:S(2)}) collective-permute-start(bf16[256,128]{1,0:T(8,128)(2,1)S(1)} %collective-permute-done.1), channel_id=1, source_target_pairs={{0,32},{8,40},{16,48},{24,56},{32,64},{40,72},{48,80},{56,88},{64,... | collective-permute-start | bytes 196616 | tf_op jit(solution)/shard_map/ppermute | solution.py:309
  48.0 8.5 %collective-permute-start.4 = (bf16[1,256,128]{2,1,0:T(8,128)(2,1)S(1)}, bf16[1,256,128]{2,1,0:T(8,128)(2,1)S(1)}, u32[]{:S(2)}, u32[]{:S(2)}) collective-permute-start(bf16[1,256,128]{2,1,0:T(8,128)(2,1)S(1)} %bitcast.9), channel_id=1, source_target_pairs={{0,1},{1,0},{2,3},{3,2},{4,5},{5,4},{6,7},{7,6},{8,9},{9,8},{10,11... | collective-permute-start | bytes 196616 | tf_op jit(solution)/shard_map/ppermute | solution.py:313
  56.5 3.9 %collective-permute-start.6 = (bf16[4,256,128]{2,1,0:T(8,128)(2,1)S(1)}, bf16[4,256,128]{2,1,0:T(8,128)(2,1)S(1)}, u32[]{:S(2)}, u32[]{:S(2)}) collective-permute-start(bf16[4,256,128]{2,1,0:T(8,128)(2,1)S(1)} %pad_maximum_fusion.refs_1_), channel_id=1, source_target_pairs={{0,1},{1,0},{2,3},{3,2},{4,5},{5,4},{6,7},{7,6},{8,9},{9,8},{10,11... | collective-permute-start | bytes 786440 | tf_op jit(solution)/shard_map/ppermute | solution.py:313
  58.5 12.7 %collective-permute-start.5 = (bf16[4,256,128]{2,1,0:T(8,128)(2,1)S(1)}, bf16[4,256,128]{2,1,0:T(8,128)(2,1)S(1)}, u32[]{:S(2)}, u32[]{:S(2)}) collective-permute-start(bf16[4,256,128]{2,1,0:T(8,128)(2,1)S(1)} %pad_maximum_fusion.refs_1_), channel_id=1, source_target_pairs={{0,8},{8,16},{16,24},{24,32},{32,40},{40,48},{48,56},{56,64},{64,7... | collective-permute-start | bytes 786440 | tf_op jit(solution)/shard_map/ppermute | solution.py:309
  71.2 3.8 %collective-permute-start.8 = (bf16[4,256,128]{2,1,0:T(8,128)(2,1)S(1)}, bf16[4,256,128]{2,1,0:T(8,128)(2,1)S(1)}, u32[]{:S(2)}, u32[]{:S(2)}) collective-permute-start(bf16[4,256,128]{2,1,0:T(8,128)(2,1)S(1)} %collective-permute-done.5.refs_2_), channel_id=1, source_target_pairs={{0,1},{1,0},{2,3},{3,2},{4,5},{5,4},{6,7},{7,6},{8,9},{9,8},{10,11... | collective-permute-start | bytes 786440 | tf_op jit(solution)/shard_map/ppermute | solution.py:313
  73.1 12.7 %collective-permute-start.7 = (bf16[4,256,128]{2,1,0:T(8,128)(2,1)S(1)}, bf16[4,256,128]{2,1,0:T(8,128)(2,1)S(1)}, u32[]{:S(2)}, u32[]{:S(2)}) collective-permute-start(bf16[4,256,128]{2,1,0:T(8,128)(2,1)S(1)} %collective-permute-done.5.refs_2_), channel_id=1, source_target_pairs={{0,8},{8,16},{16,24},{24,32},{32,40},{40,48},{48,56},{56,64},{64,7... | collective-permute-start | bytes 786440 | tf_op jit(solution)/shard_map/ppermute | solution.py:309
  85.8 16.5 %collective-permute-start.10 = (bf16[4,256,128]{2,1,0:T(8,128)(2,1)S(1)}, bf16[4,256,128]{2,1,0:T(8,128)(2,1)S(1)}, u32[]{:S(2)}, u32[]{:S(2)}) collective-permute-start(bf16[4,256,128]{2,1,0:T(8,128)(2,1)S(1)} %collective-permute-done.7.refs_0_), channel_id=1, source_target_pairs={{0,1},{1,0},{2,3},{3,2},{4,5},{5,4},{6,7},{7,6},{8,9},{9,8},{10,11... | collective-permute-start | bytes 786440 | tf_op jit(solution)/shard_map/ppermute | solution.py:313
  87.7 12.7 %collective-permute-start.9 = (bf16[4,256,128]{2,1,0:T(8,128)(2,1)S(1)}, bf16[4,256,128]{2,1,0:T(8,128)(2,1)S(1)}, u32[]{:S(2)}, u32[]{:S(2)}) collective-permute-start(bf16[4,256,128]{2,1,0:T(8,128)(2,1)S(1)} %collective-permute-done.7.refs_0_), channel_id=1, source_target_pairs={{0,8},{8,16},{16,24},{24,32},{32,40},{40,48},{48,56},{56,64},{64,7... | collective-permute-start | bytes 786440 | tf_op jit(solution)/shard_map/ppermute | solution.py:309
  89.7 14.2 %copy-start.1 = (bf16[512,2048]{1,0:T(8,128)(2,1)S(1)}, bf16[512,2048]{1,0:T(8,128)(2,1)}, u32[]{:S(2)}) copy-start(bf16[512,2048]{1,0:T(8,128)(2,1)} %refs_4_.1) | copy-start | bytes 6291460
  100.4 3.4 %collective-permute-start.11 = (bf16[4,256,128]{2,1,0:T(8,128)(2,1)S(1)}, bf16[4,256,128]{2,1,0:T(8,128)(2,1)S(1)}, u32[]{:S(2)}, u32[]{:S(2)}) collective-permute-start(bf16[4,256,128]{2,1,0:T(8,128)(2,1)S(1)} %collective-permute-done.9.refs_1_), channel_id=1, source_target_pairs={{0,1},{1,0},{2,3},{3,2},{4,5},{5,4},{6,7},{7,6},{8,9},{9,8},{10,11... | collective-permute-start | bytes 786440 | tf_op jit(solution)/shard_map/ppermute | solution.py:313
  108.6 3.8 %collective-permute-start.12 = (bf16[4,256,256]{2,1,0:T(8,128)(2,1)S(1)}, bf16[4,256,256]{2,1,0:T(8,128)(2,1)S(1)}, u32[]{:S(2)}, u32[]{:S(2)}) collective-permute-start(bf16[4,256,256]{2,1,0:T(8,128)(2,1)S(1)} %get-tuple-element.50), channel_id=1, source_target_pairs={{0,1},{1,0},{2,3},{3,2},{4,5},{5,4},{6,7},{7,6},{8,9},{9,8},{10,11... | collective-permute-start | bytes 1572872 | tf_op jit(solution)/shard_map/ppermute | solution.py:313
where the time goes:
time: 128 us; the launch traced here: 127 us
  waiting for transfers between devices  50 us (39%)
  starting transfers between devices  41.7 us (33%)
  Pallas kernels  15.8 us (12%)
  blocking collectives  13.9 us (11%)
  local copies, waits for them, and re-layouts  4.64 us (4%)
    ppermute x7, waiting for transfers between devices, passed_along(): lax.ppermute(a, 'ctx', [(i, i + distance) for i in range(n - distance)])  46.8 us
    ppermute x7, starting transfers between devices, passed_along(): lax.ppermute(a, 'ctx', [(i, i + distance) for i in range(n - distance)])  30.1 us
    all_to_all x1, blocking collectives, local(): terms = lax.all_to_all(pairs, 'x', 0, 0, tiled=True)  13.9 us
    ppermute x6, starting transfers between devices, swapped(): return lax.ppermute(a, 'c', [(0, 1), (1, 0)])  11.6 us
    pallas_call x1, Pallas kernels, attend_near(): pl.pallas_call(functools.partial(near_body, heads, n), out_shape=(state,...  6.01 us
    pallas_call x1, Pallas kernels, attend_far(): pl.pallas_call(functools.partial(far_body, heads, n), out_shape=(half, ha...  4.77 us
    unnamed x18, local copies, waits for them, and re-layouts  4.64 us
    pallas_call x1, Pallas kernels, project_kv(): pl.pallas_call(functools.partial(kv_body, heads), out_shape=(jax.ShapeDty...  4.07 us
  transfers between devices with their start and end apart: 13, of which 7 were waited for; matrix products, arithmetic and copies ran while one was open for 0% of the time, Pallas kernels for 5%

commit v1 on v0

--- a/solution.py
+++ b/solution.py
@@ -64,11 +64,14 @@
     span[0] = jnp.min(start_row).astype(jnp.int32)
     span[1] = jnp.max(start_row).astype(jnp.int32)
     offsets = (block * rows + iota((rows, 1), 0)).astype(jnp.float32) - start_column
-    angles = offsets * frequency[...]
-    cosine[...] = jnp.cos(angles)
-    lower = iota((rows, HD), 1) < HD // 2
-    turned = jnp.sin(angles)
-    sine[...] = jnp.where(lower, -turned, turned)
+    half = rows // 2
+    lower = iota((half, HD), 1) < HD // 2
+    angles = jnp.where(lower, offsets[:half], offsets[half:]) * frequency[...]
+    for table, wave in ((cosine, jnp.cos(angles)), (sine, jnp.sin(angles))):
+        other = pltpu.roll(wave, HD // 2, 1)
+        sign = -1.0 if table is sine else 1.0
+        table[:half] = jnp.where(lower, sign * wave, other)
+        table[half:] = jnp.where(lower, sign * other, wave)
 
     tokens_copy.wait()
     pltpu.make_async_copy(w_key.at[:, columns], weight, sems.at[1]).wait()
@@ -113,25 +116,58 @@
     )(tokens, w_key, w_value, gain, lengths, frequency)
 
 
-def q_body(heads, tokens, w_query, gain, cosine, sine, out):
-    u = jnp.dot(tokens[...], w_query[...], preferred_element_type=jnp.float32)
-    for h in range(heads):
-        part = u[:, h * HD : (h + 1) * HD]
-        out[h] = norm_rotate(part, gain[...], cosine[...], sine[...]).astype(out.dtype)
+def q_body(tokens_hbm, w_hbm, gain, cosine_any, sine_any, out, tokens, weight, cosine, sine, sems):
+    wide = weight.shape[2]
+    copies = [
+        pltpu.make_async_copy(tokens_hbm, tokens, sems.at[0]),
+        pltpu.make_async_copy(w_hbm.at[:, pl.ds(0, wide)], weight.at[0], sems.at[1]),
+        pltpu.make_async_copy(cosine_any, cosine, sems.at[2]),
+        pltpu.make_async_copy(sine_any, sine, sems.at[3]),
+    ]
+    later = []
+    for i in range(1, weight.shape[0]):
+        later.append(
+            pltpu.make_async_copy(
+                w_hbm.at[:, pl.ds(i * wide, wide)], weight.at[i], sems.at[3 + i]
+            )
+        )
+    for copy in copies + later:
+        copy.start()
+    for copy in copies:
+        copy.wait()
+    each = wide // HD
+    for i in range(weight.shape[0]):
+        if i > 0:
+            later[i - 1].wait()
+        u = jnp.dot(tokens[...], weight[i], preferred_element_type=jnp.float32)
+        for h in range(each):
+            part = u[:, h * HD : (h + 1) * HD]
+            turned = norm_rotate(part, gain[...], cosine[...], sine[...])
+            out[i * each + h] = turned.astype(out.dtype)
 
 
 def project_q(tokens, w_query, gain, cosine, sine):
     rows, width = tokens.shape
     heads = w_query.shape[1] // HD
+    chunks = 2
     return pl.pallas_call(
-        functools.partial(q_body, heads),
+        q_body,
         out_shape=jax.ShapeDtypeStruct((heads, rows, HD), jnp.bfloat16),
-        in_specs=[pl.BlockSpec(memory_space=VMEM)] * 5,
+        in_specs=[pl.BlockSpec(memory_space=pltpu.HBM)] * 2
+        + [pl.BlockSpec(memory_space=VMEM)]
+        + [pl.BlockSpec(memory_space=pl.ANY)] * 2,
         out_specs=pl.BlockSpec(memory_space=VMEM),
+        scratch_shapes=[
+            VMEM((rows, width), tokens.dtype),
+            VMEM((chunks, width, heads * HD // chunks), w_query.dtype),
+            VMEM((rows, HD), jnp.float32),
+            VMEM((rows, HD), jnp.float32),
+            pltpu.SemaphoreType.DMA((3 + chunks,)),
+        ],
         cost_estimate=pl.CostEstimate(
             flops=2 * rows * width * heads * HD, bytes_accessed=6 * rows * width, transcendentals=0
         ),
-        compiler_params=pltpu.CompilerParams(vmem_limit_bytes=10 << 20),
+        compiler_params=pltpu.CompilerParams(vmem_limit_bytes=63 << 20),
         name="project_q",
     )(tokens, w_query, gain, cosine, sine)
 
@@ -321,21 +357,18 @@
     )
     own = part[None]
     far = [passed_along(part, LINE + 1)]
-    far.append(passed_along(far[-1], LINE))
+    near = passed_along(part, 1)
+    theirs = [swapped(own)]
+    for _ in range(2):
+        far.append(passed_along(far[-1], LINE))
     queries = project_q(tokens, w_query, query_gain[None], cosine, sine)
-    middle, queries = lax.optimization_barrier((far[-1], queries))
-    far.append(passed_along(middle, LINE))
-    hops = [jnp.stack([passed_along(part, 1)] + far)]
-    theirs = [swapped(own)]
+    hops = [jnp.stack([near] + far)]
     for _ in range(LINE - 1):
-        hop, theirs = lax.optimization_barrier((hops[-1], theirs))
-        hops.append(passed_along(hop, 1))
-        theirs = theirs + [swapped(hop)]
+        hops.append(passed_along(hops[-1], 1))
+        theirs = theirs + [swapped(hops[-2])]
     mine = [own] + hops
-
-    state = attend_near(span, queries, starts, mine[:3], theirs[:3])
-    last, (total, weighted) = lax.optimization_barrier((hops[-1], state))
-    theirs.append(swapped(last))
+    total, weighted = attend_near(span, queries, starts, mine[:3], theirs[:3])
+    theirs.append(swapped(hops[-1]))
     keep, give = attend_far(
         span, queries, starts, total, weighted, mine[3:], theirs[3:], w_out, chips
     )

time: 128 us -> 127 us (level)
  waiting for transfers between devices: 50 us -> 45.6 us
  Pallas kernels: 15.8 us -> 19.8 us
  local copies, waits for them, and re-layouts: 4.64 us -> 1.8 us
  starting transfers between devices: 41.7 us -> 43.9 us
    pallas_call x1, Pallas kernels: 0.99 us -> 4.67 us  [project_q(): pl.pallas_call(q_body, out_shape=jax.ShapeDtypeStruct((heads, rows, HD),...]
    unnamed x18 -> x12, local copies, waits for them, and re-layouts: 4.64 us -> 1.8 us
    ppermute x7, waiting for transfers between devices: 46.8 us -> 44.1 us  [passed_along(): lax.ppermute(a, 'ctx', [(i, i + distance) for i in range(n - distance)])]
    ppermute x6, waiting for transfers between devices: 3.24 us -> 1.53 us  [swapped(): return lax.ppermute(a, 'c', [(0, 1), (1, 0)])]
    ppermute x6, starting transfers between devices: 11.6 us -> 13 us  [swapped(): return lax.ppermute(a, 'c', [(0, 1), (1, 0)])]
  transfers between devices with their start and end apart: 13 -> 13, of which waited for: 7 -> 6; matrix products, arithmetic and copies ran while one was open for 0% -> 0% of each run, Pallas kernels for 5% -> 9%
where the time goes in v1:
time: 127 us; the launch traced here: 126 us
  waiting for transfers between devices  45.6 us (36%)
  starting transfers between devices  43.9 us (35%)
  Pallas kernels  19.8 us (16%)
  blocking collectives  14.1 us (11%)
  local copies, waits for them, and re-layouts  1.8 us (1%)
    ppermute x7, waiting for transfers between devices, passed_along(): lax.ppermute(a, 'ctx', [(i, i + distance) for i in range(n - distance)])  44.1 us
    ppermute x7, starting transfers between devices, passed_along(): lax.ppermute(a, 'ctx', [(i, i + distance) for i in range(n - distance)])  30.9 us
    all_to_all x1, blocking collectives, local(): terms = lax.all_to_all(pairs, 'x', 0, 0, tiled=True)  14.1 us
    ppermute x6, starting transfers between devices, swapped(): return lax.ppermute(a, 'c', [(0, 1), (1, 0)])  13 us
    pallas_call x1, Pallas kernels, attend_near(): pl.pallas_call(functools.partial(near_body, heads, n), out_shape=(state,...  6.91 us
    pallas_call x1, Pallas kernels, attend_far(): pl.pallas_call(functools.partial(far_body, heads, n), out_shape=(half, ha...  4.75 us
    pallas_call x1, Pallas kernels, project_q(): pl.pallas_call(q_body, out_shape=jax.ShapeDtypeStruct((heads, rows, HD),...  4.67 us
    pallas_call x1, Pallas kernels, project_kv(): pl.pallas_call(functools.partial(kv_body, heads), out_shape=(jax.ShapeDty...  3.5 us
  transfers between devices with their start and end apart: 13, of which 6 were waited for; matrix products, arithmetic and copies ran while one was open for 0% of the time, Pallas kernels for 9%

profile of v1, /device:TPU:24, one launch (start us, length us, event | category | flops | bytes accessed | tf_op | source)
XLA Modules:
  0.0 126.4 jit_solution(12611417686831422576)
XLA Ops:
  0.0 3.5 %project_kv.1 = (bf16[256,128]{1,0:T(8,128)(2,1)}, f32[256,128]{1,0:T(8,128)}, f32[256,128]{1,0:T(8,128)}, s32[256,1]{1,0:T(8,128)}, s32[2]{0:T(128)}) custom-call(bf16[256,2048]{1,0:T(8,128)(2,1)} %tokens_hbm.3, bf16[2048,512]{1,0:T(8,128)(2,1)} %w_key.1, bf16[2048,512]{1,0:T(8,128)(2,1)} %w_value.1, f32[1,128]{1,0:T(1,128)} %bitcast.15, ...), custom_call_target="tpu_custom_call" | custom-call | flops 134217728 | bytes 2097152 | tf_op jit(solution)/shard_map/project_kv/pallas_call | solution.py:93
  3.5 10.5 %collective-permute-start.1 = (bf16[256,128]{1,0:T(8,128)(2,1)}, bf16[256,128]{1,0:T(8,128)(2,1)S(1)}, u32[]{:S(2)}, u32[]{:S(2)}) collective-permute-start(bf16[256,128]{1,0:T(8,128)(2,1)} %get-tuple-element.18), channel_id=1, source_target_pairs={{0,40},{8,48},{16,56},{24,64},{32,72},{40,80},{48,88},{56,96},{64,... | collective-permute-start | bytes 196616 | tf_op jit(solution)/shard_map/ppermute | solution.py:345
  14.0 13.9 %collective-permute-done.1 = bf16[256,128]{1,0:T(8,128)(2,1)S(1)} collective-permute-done((bf16[256,128]{1,0:T(8,128)(2,1)}, bf16[256,128]{1,0:T(8,128)(2,1)S(1)}, u32[]{:S(2)}, u32[]{:S(2)}) %collective-permute-start.1) | collective-permute-done | bytes 65568 | tf_op jit(solution)/shard_map/ppermute | solution.py:345
  27.9 9.5 %collective-permute-start.2 = (bf16[256,128]{1,0:T(8,128)(2,1)S(1)}, bf16[256,128]{1,0:T(8,128)(2,1)S(1)}, u32[]{:S(2)}, u32[]{:S(2)}) collective-permute-start(bf16[256,128]{1,0:T(8,128)(2,1)S(1)} %collective-permute-done.1), channel_id=1, source_target_pairs={{0,32},{8,40},{16,48},{24,56},{32,64},{40,72},{48,80},{56,88},{64,... | collective-permute-start | bytes 196616 | tf_op jit(solution)/shard_map/ppermute | solution.py:345
  37.4 1.9 %collective-permute-start = (bf16[256,128]{1,0:T(8,128)(2,1)}, bf16[256,128]{1,0:T(8,128)(2,1)S(1)}, u32[]{:S(2)}, u32[]{:S(2)}) collective-permute-start(bf16[256,128]{1,0:T(8,128)(2,1)} %get-tuple-element.18), channel_id=1, source_target_pairs={{0,8},{8,16},{16,24},{24,32},{32,40},{40,48},{48,56},{56,64},{64,7... | collective-permute-start | bytes 196616 | tf_op jit(solution)/shard_map/ppermute | solution.py:345
  39.3 5.2 %collective-permute-done.2 = bf16[256,128]{1,0:T(8,128)(2,1)S(1)} collective-permute-done((bf16[256,128]{1,0:T(8,128)(2,1)S(1)}, bf16[256,128]{1,0:T(8,128)(2,1)S(1)}, u32[]{:S(2)}, u32[]{:S(2)}) %collective-permute-start.2) | collective-permute-done | bytes 65568 | tf_op jit(solution)/shard_map/ppermute | solution.py:345
  44.5 3.0 %collective-permute-start.3 = (bf16[256,128]{1,0:T(8,128)(2,1)S(1)}, bf16[256,128]{1,0:T(8,128)(2,1)S(1)}, u32[]{:S(2)}, u32[]{:S(2)}) collective-permute-start(bf16[256,128]{1,0:T(8,128)(2,1)S(1)} %collective-permute-done.2), channel_id=1, source_target_pairs={{0,32},{8,40},{16,48},{24,56},{32,64},{40,72},{48,80},{56,88},{64,... | collective-permute-start | bytes 196616 | tf_op jit(solution)/shard_map/ppermute | solution.py:345
  47.4 0.0 collective-permute-done
  47.4 8.0 %collective-permute-done.3 = bf16[256,128]{1,0:T(8,128)(2,1)S(1)} collective-permute-done((bf16[256,128]{1,0:T(8,128)(2,1)S(1)}, bf16[256,128]{1,0:T(8,128)(2,1)S(1)}, u32[]{:S(2)}, u32[]{:S(2)}) %collective-permute-start.3) | collective-permute-done | bytes 65568 | tf_op jit(solution)/shard_map/ppermute | solution.py:345
  55.4 0.0 copy-start.3
  55.4 0.0 copy-start.4
  55.5 2.3 %collective-permute-start.4 = (bf16[4,256,128]{2,1,0:T(8,128)(2,1)S(1)}, bf16[4,256,128]{2,1,0:T(8,128)(2,1)}, u32[]{:S(2)}, u32[]{:S(2)}) collective-permute-start(bf16[4,256,128]{2,1,0:T(8,128)(2,1)S(1)} %pad_maximum_fusion.refs_1_), channel_id=1, source_target_pairs={{0,8},{8,16},{16,24},{24,32},{32,40},{40,48},{48,56},{56,64},{64,7... | collective-permute-start | bytes 786440 | tf_op jit(solution)/shard_map/ppermute | solution.py:345
  57.8 8.3 %collective-permute-done.4.refs_2_ = bf16[4,256,128]{2,1,0:T(8,128)(2,1)} collective-permute-done((bf16[4,256,128]{2,1,0:T(8,128)(2,1)S(1)}, bf16[4,256,128]{2,1,0:T(8,128)(2,1)}, u32[]{:S(2)}, u32[]{:S(2)}) %collective-permute-start.4) | collective-permute-done | bytes 262176 | tf_op jit(solution)/shard_map/ppermute | solution.py:345
  66.1 1.9 %collective-permute-start.8 = (bf16[4,256,128]{2,1,0:T(8,128)(2,1)}, bf16[4,256,128]{2,1,0:T(8,128)(2,1)S(1)}, u32[]{:S(2)}, u32[]{:S(2)}) collective-permute-start(bf16[4,256,128]{2,1,0:T(8,128)(2,1)} %collective-permute-done.4.refs_2_), channel_id=1, source_target_pairs={{0,8},{8,16},{16,24},{24,32},{32,40},{40,48},{48,56},{56,64},{64,7... | collective-permute-start | bytes 786440 | tf_op jit(solution)/shard_map/ppermute | solution.py:345
  68.0 8.7 %collective-permute-done.8.refs_0_ = bf16[4,256,128]{2,1,0:T(8,128)(2,1)S(1)} collective-permute-done((bf16[4,256,128]{2,1,0:T(8,128)(2,1)}, bf16[4,256,128]{2,1,0:T(8,128)(2,1)S(1)}, u32[]{:S(2)}, u32[]{:S(2)}) %collective-permute-start.8) | collective-permute-done | bytes 262176 | tf_op jit(solution)/shard_map/ppermute | solution.py:345
  76.7 1.9 %collective-permute-start.9 = (bf16[4,256,128]{2,1,0:T(8,128)(2,1)S(1)}, bf16[4,256,128]{2,1,0:T(8,128)(2,1)S(1)}, u32[]{:S(2)}, u32[]{:S(2)}) collective-permute-start(bf16[4,256,128]{2,1,0:T(8,128)(2,1)S(1)} %collective-permute-done.8.refs_0_), channel_id=1, source_target_pairs={{0,8},{8,16},{16,24},{24,32},{32,40},{40,48},{48,56},{56,64},{64,7... | collective-permute-start | bytes 786440 | tf_op jit(solution)/shard_map/ppermute | solution.py:345
  78.6 1.9 %collective-permute-start.6 = (bf16[4,256,128]{2,1,0:T(8,128)(2,1)S(1)}, bf16[4,256,128]{2,1,0:T(8,128)(2,1)}, u32[]{:S(2)}, u32[]{:S(2)}) collective-permute-start(bf16[4,256,128]{2,1,0:T(8,128)(2,1)S(1)} %pad_maximum_fusion.refs_1_), channel_id=1, source_target_pairs={{0,1},{1,0},{2,3},{3,2},{4,5},{5,4},{6,7},{7,6},{8,9},{9,8},{10,11... | collective-permute-start | bytes 786440 | tf_op jit(solution)/shard_map/ppermute | solution.py:349
  80.5 2.4 %collective-permute-start.7 = (bf16[4,256,128]{2,1,0:T(8,128)(2,1)}, bf16[4,256,128]{2,1,0:T(8,128)(2,1)}, u32[]{:S(2)}, u32[]{:S(2)}) collective-permute-start(bf16[4,256,128]{2,1,0:T(8,128)(2,1)} %collective-permute-done.4.refs_2_), channel_id=1, source_target_pairs={{0,1},{1,0},{2,3},{3,2},{4,5},{5,4},{6,7},{7,6},{8,9},{9,8},{10,11... | collective-permute-start | bytes 786440 | tf_op jit(solution)/shard_map/ppermute | solution.py:349
  82.9 1.9 %collective-permute-start.5 = (bf16[1,256,128]{2,1,0:T(8,128)(2,1)}, bf16[1,256,128]{2,1,0:T(8,128)(2,1)}, u32[]{:S(2)}, u32[]{:S(2)}) collective-permute-start(bf16[1,256,128]{2,1,0:T(8,128)(2,1)} %bitcast.8), channel_id=1, source_target_pairs={{0,1},{1,0},{2,3},{3,2},{4,5},{5,4},{6,7},{7,6},{8,9},{9,8},{10,11... | collective-permute-start | bytes 196616 | tf_op jit(solution)/shard_map/ppermute | solution.py:349
  84.9 4.7 %project_q.1.queries = bf16[4,256,128]{2,1,0:T(8,128)(2,1)} custom-call(bf16[256,2048]{1,0:T(8,128)(2,1)} %tokens_hbm.3, bf16[2048,512]{1,0:T(8,128)(2,1)} %w_hbm.1, f32[1,128]{1,0:T(1,128)} %bitcast.16, f32[256,128]{1,0:T(8,128)} %get-tuple-element.15.cosine_any, f32[256,128]{1,0:T(8,128)} %get-tuple-element.16.sine_any), custom_call_target="tpu_custom_call" | custom-call | flops 536870912 | bytes 3145728 | tf_op jit(solution)/shard_map/project_q/pallas_call | solution.py:153
  89.5 2.4 %collective-permute-start.10 = (bf16[4,256,128]{2,1,0:T(8,128)(2,1)S(1)}, bf16[4,256,128]{2,1,0:T(8,128)(2,1)S(1)}, u32[]{:S(2)}, u32[]{:S(2)}) collective-permute-start(bf16[4,256,128]{2,1,0:T(8,128)(2,1)S(1)} %collective-permute-done.8.refs_0_), channel_id=1, source_target_pairs={{0,1},{1,0},{2,3},{3,2},{4,5},{5,4},{6,7},{7,6},{8,9},{9,8},{10,11... | collective-permute-start | bytes 786440 | tf_op jit(solution)/shard_map/ppermute | solution.py:349
  91.9 0.0 collective-permute-done.9.refs_1_
  92.0 1.9 %collective-permute-start.11 = (bf16[4,256,128]{2,1,0:T(8,128)(2,1)S(1)}, bf16[4,256,128]{2,1,0:T(8,128)(2,1)S(1)}, u32[]{:S(2)}, u32[]{:S(2)}) collective-permute-start(bf16[4,256,128]{2,1,0:T(8,128)(2,1)S(1)} %collective-permute-done.9.refs_1_), channel_id=1, source_target_pairs={{0,1},{1,0},{2,3},{3,2},{4,5},{5,4},{6,7},{7,6},{8,9},{9,8},{10,11... | collective-permute-start | bytes 786440 | tf_op jit(solution)/shard_map/ppermute | solution.py:349
  93.9 0.0 collective-permute-done.5.refs_3_
  93.9 0.0 collective-permute-done.6.refs_4_
  93.9 0.0 collective-permute-done.7.refs_5_
  93.9 0.0 copy-done.3
  93.9 0.0 copy-done.4
  93.9 0.0 copy-start.1
  94.0 0.9 copy-done.1
  94.9 0.0 copy-start.5
  94.9 0.8 copy-done.5
  95.7 0.0 copy-start
  95.7 0.0 copy-start.2
  95.7 6.9 %attend_near.1 = (f32[4,256,128]{2,1,0:T(8,128)S(1)}, f32[4,256,128]{2,1,0:T(8,128)S(1)}) custom-call(s32[2]{0:T(128)S(1)} %copy-done.4, bf16[4,256,128]{2,1,0:T(8,128)(2,1)S(1)} %copy-done.1, s32[256,1]{1,0:T(8,128)S(1)} %copy-done.3, bf16[1,256,128]{2,1,0:T(8,128)(2,1)S(1)} %bitcast.9, bf16[4,256,128]{2,1,0:T(8,128)(2,1)S(1)} %pad_maximum_fusion.refs_1_, ...), custom_call_target="tpu_custom_call" | custom-call | flops 4831838208 | bytes 2097152 | tf_op jit(solution)/shard_map/attend_near/pallas_call | solution.py:262
  102.7 0.0 collective-permute-done.10.refs_2_
  102.7 0.0 collective-permute-done.11.refs_3_
  102.7 0.0 copy-done
  102.7 0.0 copy-done.2
  102.7 4.7 %attend_far.1 = (bf16[4,256,256]{2,1,0:T(8,128)(2,1)S(1)}, bf16[4,256,256]{2,1,0:T(8,128)(2,1)S(1)}) custom-call(s32[2]{0:T(128)S(1)} %copy-done.4, bf16[4,256,128]{2,1,0:T(8,128)(2,1)S(1)} %copy-done.2, s32[256,1]{1,0:T(8,128)S(1)} %copy-done.3, f32[4,256,128]{2,1,0:T(8,128)S(1)} %get-tuple-element.19.total_in, ...), custom_call_target="tpu_custom_call" | custom-call | flops 1073741824 | bytes 4194304 | tf_op jit(solution)/shard_map/attend_far/pallas_call | solution.py:319
  107.4 2.4 %collective-permute-start.12 = (bf16[4,256,256]{2,1,0:T(8,128)(2,1)S(1)}, bf16[4,256,256]{2,1,0:T(8,128)(2,1)S(1)}, u32[]{:S(2)}, u32[]{:S(2)}) collective-permute-start(bf16[4,256,256]{2,1,0:T(8,128)(2,1)S(1)} %get-tuple-element.22), channel_id=1, source_target_pairs={{0,1},{1,0},{2,3},{3,2},{4,5},{5,4},{6,7},{7,6},{8,9},{9,8},{10,11... | collective-permute-start | bytes 1572872 | tf_op jit(solution)/shard_map/ppermute | solution.py:349
  109.8 1.5 %collective-permute-done.12 = bf16[4,256,256]{2,1,0:T(8,128)(2,1)S(1)} collective-permute-done((bf16[4,256,256]{2,1,0:T(8,128)(2,1)S(1)}, bf16[4,256,256]{2,1,0:T(8,128)(2,1)S(1)}, u32[]{:S(2)}, u32[]{:S(2)}) %collective-permute-start.12) | collective-permute-done | bytes 524320 | tf_op jit(solution)/shard_map/ppermute | solution.py:349
  111.4 0.1 add_convert_fusion
  111.5 14.1 %all_to_all.5 = bf16[4,256,256]{2,1,0:T(8,128)(2,1)S(1)} all-to-all(bf16[4,256,256]{2,1,0:T(8,128)(2,1)S(1)} %add_convert_fusion), channel_id=1, replica_groups=mesh['ctx'=128,'x'=4,'c'=2] {'x'}, dimensions={0} | all-to-all | bytes 1048576 | tf_op jit(solution)/shard_map/all_to_all | solution.py:376
  125.6 0.7 reduce_sum.12
  (1 shorter events, 0.0 us)
Async XLA Ops:
  3.5 24.4 %collective-permute-start.1 = (bf16[256,128]{1,0:T(8,128)(2,1)}, bf16[256,128]{1,0:T(8,128)(2,1)S(1)}, u32[]{:S(2)}, u32[]{:S(2)}) collective-permute-start(bf16[256,128]{1,0:T(8,128)(2,1)} %get-tuple-element.18), channel_id=1, source_target_pairs={{0,40},{8,48},{16,56},{24,64},{32,72},{40,80},{48,88},{56,96},{64,... | collective-permute-start | bytes 196616 | tf_op jit(solution)/shard_map/ppermute | solution.py:345
  27.9 16.5 %collective-permute-start.2 = (bf16[256,128]{1,0:T(8,128)(2,1)S(1)}, bf16[256,128]{1,0:T(8,128)(2,1)S(1)}, u32[]{:S(2)}, u32[]{:S(2)}) collective-permute-start(bf16[256,128]{1,0:T(8,128)(2,1)S(1)} %collective-permute-done.1), channel_id=1, source_target_pairs={{0,32},{8,40},{16,48},{24,56},{32,64},{40,72},{48,80},{56,88},{64,... | collective-permute-start | bytes 196616 | tf_op jit(solution)/shard_map/ppermute | solution.py:345
  37.4 10.1 %collective-permute-start = (bf16[256,128]{1,0:T(8,128)(2,1)}, bf16[256,128]{1,0:T(8,128)(2,1)S(1)}, u32[]{:S(2)}, u32[]{:S(2)}) collective-permute-start(bf16[256,128]{1,0:T(8,128)(2,1)} %get-tuple-element.18), channel_id=1, source_target_pairs={{0,8},{8,16},{16,24},{24,32},{32,40},{40,48},{48,56},{56,64},{64,7... | collective-permute-start | bytes 196616 | tf_op jit(solution)/shard_map/ppermute | solution.py:345
  44.5 11.0 %collective-permute-start.3 = (bf16[256,128]{1,0:T(8,128)(2,1)S(1)}, bf16[256,128]{1,0:T(8,128)(2,1)S(1)}, u32[]{:S(2)}, u32[]{:S(2)}) collective-permute-start(bf16[256,128]{1,0:T(8,128)(2,1)S(1)} %collective-permute-done.2), channel_id=1, source_target_pairs={{0,32},{8,40},{16,48},{24,56},{32,64},{40,72},{48,80},{56,88},{64,... | collective-permute-start | bytes 196616 | tf_op jit(solution)/shard_map/ppermute | solution.py:345
  55.4 38.5 %copy-start.3 = (s32[256,1]{1,0:T(8,128)S(1)}, s32[256,1]{1,0:T(8,128)}, u32[]{:S(2)}) copy-start(s32[256,1]{1,0:T(8,128)} %get-tuple-element.17.starts) | copy-start | bytes 3076
  55.4 38.5 %copy-start.4 = (s32[2]{0:T(128)S(1)}, s32[2]{0:T(128)}, u32[]{:S(2)}) copy-start(s32[2]{0:T(128)} %get-tuple-element.14.span) | copy-start | bytes 28
  55.5 10.6 %collective-permute-start.4 = (bf16[4,256,128]{2,1,0:T(8,128)(2,1)S(1)}, bf16[4,256,128]{2,1,0:T(8,128)(2,1)}, u32[]{:S(2)}, u32[]{:S(2)}) collective-permute-start(bf16[4,256,128]{2,1,0:T(8,128)(2,1)S(1)} %pad_maximum_fusion.refs_1_), channel_id=1, source_target_pairs={{0,8},{8,16},{16,24},{24,32},{32,40},{40,48},{48,56},{56,64},{64,7... | collective-permute-start | bytes 786440 | tf_op jit(solution)/shard_map/ppermute | solution.py:345
  66.1 10.6 %collective-permute-start.8 = (bf16[4,256,128]{2,1,0:T(8,128)(2,1)}, bf16[4,256,128]{2,1,0:T(8,128)(2,1)S(1)}, u32[]{:S(2)}, u32[]{:S(2)}) collective-permute-start(bf16[4,256,128]{2,1,0:T(8,128)(2,1)} %collective-permute-done.4.refs_2_), channel_id=1, source_target_pairs={{0,8},{8,16},{16,24},{24,32},{32,40},{40,48},{48,56},{56,64},{64,7... | collective-permute-start | bytes 786440 | tf_op jit(solution)/shard_map/ppermute | solution.py:345
  76.7 15.3 %collective-permute-start.9 = (bf16[4,256,128]{2,1,0:T(8,128)(2,1)S(1)}, bf16[4,256,128]{2,1,0:T(8,128)(2,1)S(1)}, u32[]{:S(2)}, u32[]{:S(2)}) collective-permute-start(bf16[4,256,128]{2,1,0:T(8,128)(2,1)S(1)} %collective-permute-done.8.refs_0_), channel_id=1, source_target_pairs={{0,8},{8,16},{16,24},{24,32},{32,40},{40,48},{48,56},{56,64},{64,7... | collective-permute-start | bytes 786440 | tf_op jit(solution)/shard_map/ppermute | solution.py:345
  78.6 15.3 %collective-permute-start.6 = (bf16[4,256,128]{2,1,0:T(8,128)(2,1)S(1)}, bf16[4,256,128]{2,1,0:T(8,128)(2,1)}, u32[]{:S(2)}, u32[]{:S(2)}) collective-permute-start(bf16[4,256,128]{2,1,0:T(8,128)(2,1)S(1)} %pad_maximum_fusion.refs_1_), channel_id=1, source_target_pairs={{0,1},{1,0},{2,3},{3,2},{4,5},{5,4},{6,7},{7,6},{8,9},{9,8},{10,11... | collective-permute-start | bytes 786440 | tf_op jit(solution)/shard_map/ppermute | solution.py:349
  80.5 13.4 %collective-permute-start.7 = (bf16[4,256,128]{2,1,0:T(8,128)(2,1)}, bf16[4,256,128]{2,1,0:T(8,128)(2,1)}, u32[]{:S(2)}, u32[]{:S(2)}) collective-permute-start(bf16[4,256,128]{2,1,0:T(8,128)(2,1)} %collective-permute-done.4.refs_2_), channel_id=1, source_target_pairs={{0,1},{1,0},{2,3},{3,2},{4,5},{5,4},{6,7},{7,6},{8,9},{9,8},{10,11... | collective-permute-start | bytes 786440 | tf_op jit(solution)/shard_map/ppermute | solution.py:349
  82.9 11.0 %collective-permute-start.5 = (bf16[1,256,128]{2,1,0:T(8,128)(2,1)}, bf16[1,256,128]{2,1,0:T(8,128)(2,1)}, u32[]{:S(2)}, u32[]{:S(2)}) collective-permute-start(bf16[1,256,128]{2,1,0:T(8,128)(2,1)} %bitcast.8), channel_id=1, source_target_pairs={{0,1},{1,0},{2,3},{3,2},{4,5},{5,4},{6,7},{7,6},{8,9},{9,8},{10,11... | collective-permute-start | bytes 196616 | tf_op jit(solution)/shard_map/ppermute | solution.py:349
  89.5 13.1 %collective-permute-start.10 = (bf16[4,256,128]{2,1,0:T(8,128)(2,1)S(1)}, bf16[4,256,128]{2,1,0:T(8,128)(2,1)S(1)}, u32[]{:S(2)}, u32[]{:S(2)}) collective-permute-start(bf16[4,256,128]{2,1,0:T(8,128)(2,1)S(1)} %collective-permute-done.8.refs_0_), channel_id=1, source_target_pairs={{0,1},{1,0},{2,3},{3,2},{4,5},{5,4},{6,7},{7,6},{8,9},{9,8},{10,11... | collective-permute-start | bytes 786440 | tf_op jit(solution)/shard_map/ppermute | solution.py:349
  92.0 10.7 %collective-permute-start.11 = (bf16[4,256,128]{2,1,0:T(8,128)(2,1)S(1)}, bf16[4,256,128]{2,1,0:T(8,128)(2,1)S(1)}, u32[]{:S(2)}, u32[]{:S(2)}) collective-permute-start(bf16[4,256,128]{2,1,0:T(8,128)(2,1)S(1)} %collective-permute-done.9.refs_1_), channel_id=1, source_target_pairs={{0,1},{1,0},{2,3},{3,2},{4,5},{5,4},{6,7},{7,6},{8,9},{9,8},{10,11... | collective-permute-start | bytes 786440 | tf_op jit(solution)/shard_map/ppermute | solution.py:349
  93.9 1.0 copy-start.1
  94.9 0.8 copy-start.5
  95.7 6.9 %copy-start = (bf16[512,2048]{1,0:T(8,128)(2,1)S(1)}, bf16[512,2048]{1,0:T(8,128)(2,1)}, u32[]{:S(2)}) copy-start(bf16[512,2048]{1,0:T(8,128)(2,1)} %refs_4_.1) | copy-start | bytes 6291460
  95.7 7.0 %copy-start.2 = (bf16[4,256,128]{2,1,0:T(8,128)(2,1)S(1)}, bf16[4,256,128]{2,1,0:T(8,128)(2,1)}, u32[]{:S(2)}) copy-start(bf16[4,256,128]{2,1,0:T(8,128)(2,1)} %project_q.1.queries) | copy-start | bytes 786436
  107.4 3.9 %collective-permute-start.12 = (bf16[4,256,256]{2,1,0:T(8,128)(2,1)S(1)}, bf16[4,256,256]{2,1,0:T(8,128)(2,1)S(1)}, u32[]{:S(2)}, u32[]{:S(2)}) collective-permute-start(bf16[4,256,256]{2,1,0:T(8,128)(2,1)S(1)} %get-tuple-element.22), channel_id=1, source_target_pairs={{0,1},{1,0},{2,3},{3,2},{4,5},{5,4},{6,7},{7,6},{8,9},{9,8},{10,11... | collective-permute-start | bytes 1572872 | tf_op jit(solution)/shard_map/ppermute | solution.py:349

commit v2 on v1

--- a/solution.py
+++ b/solution.py
@@ -172,22 +172,32 @@
     )(tokens, w_query, gain, cosine, sine)
 
 
+def scored(query, key):
+    return lax.dot_general(
+        query, key, (((1,), (1,)), ((), ())), preferred_element_type=jnp.float32
+    )
+
+
 def add_block(heads, queries, key, value, total, weighted, mask):
+    scores = scored(queries[0], key)
     for h in range(heads):
-        scores = lax.dot_general(
-            queries[h], key, (((1,), (1,)), ((), ())), preferred_element_type=jnp.float32
-        )
+        following = scored(queries[h + 1], key) if h + 1 < heads else None
         weights = jnp.exp2(scores * (HD**-0.5 * LOG2E))
         if mask is not None:
             weights = weights * mask[...]
-        total[h] += weights[:, :HD] + weights[:, HD:]
+        sums = weights[:, :HD]
+        for at in range(HD, weights.shape[1], HD):
+            sums = sums + weights[:, at : at + HD]
+        total[h] += sums
         weighted[h] += jnp.dot(
             weights.astype(jnp.bfloat16), value, preferred_element_type=jnp.float32
         )
-
-
-def add_blocks(heads, distance_of, places, span, queries, starts, kv, total, weighted, mask):
+        scores = following
+
+
+def add_blocks(heads, distance_of, deepest, span, queries, starts, kv, total, weighted, mask):
     rows = queries.shape[1]
+    places = kv.shape[1]
     block = lax.axis_index("ctx")
     first = span[0] // rows
     last = span[1]
@@ -214,7 +224,16 @@
 
         return carry
 
-    lax.fori_loop(0, places, step, 0)
+    together = (block - deepest) * rows >= last
+
+    @pl.when(together)
+    def _():
+        four = pl.ds(places - LINE, LINE)
+        key = kv[0, four].reshape(LINE * rows, HD)
+        value = kv[1, four].reshape(LINE * rows, HD)
+        add_block(heads, queries, key, value, total, weighted, None)
+
+    lax.fori_loop(0, jnp.where(together, places - LINE, places), step, 0)
 
 
 def start_copies(mine, theirs, kv, sems):
@@ -235,35 +254,35 @@
     return copies
 
 
-def near_body(heads, n, span, queries, starts, *refs):
+def near_body(heads, first_call, distance_of, deepest, n, span, queries, starts, *refs):
+    if not first_call:
+        total_in, weighted_in, refs = refs[0], refs[1], refs[2:]
     mine, theirs = refs[:n], refs[n : 2 * n]
     total, weighted, mask, kv, sems = refs[2 * n :]
     copies = start_copies(mine, theirs, kv, sems)
-    total[...] = jnp.zeros_like(total)
-    weighted[...] = jnp.zeros_like(weighted)
+    if first_call:
+        total[...] = jnp.zeros_like(total)
+        weighted[...] = jnp.zeros_like(weighted)
+    else:
+        total[...] = total_in[...]
+        weighted[...] = weighted_in[...]
     for copy in copies:
         copy.wait()
-
-    def distance_of(place):
-        return jnp.where(
-            place == 0, 0, 1 + (place - 1) // LINE + LINE * ((place - 1 + LINE) % LINE)
-        )
-
     add_blocks(
-        heads, distance_of, kv.shape[1], span, queries, starts, kv, total, weighted, mask
-    )
-
-
-def attend_near(span, queries, starts, mine, theirs):
+        heads, distance_of, deepest, span, queries, starts, kv, total, weighted, mask
+    )
+
+
+def attend_near(span, queries, starts, state, mine, theirs, distance_of, deepest):
     heads, rows, _ = queries.shape
     n = len(mine)
     places = sum(a.shape[0] for a in mine)
-    state = jax.ShapeDtypeStruct((heads, rows, HD), jnp.float32)
+    shape = jax.ShapeDtypeStruct((heads, rows, HD), jnp.float32)
     return pl.pallas_call(
-        functools.partial(near_body, heads, n),
-        out_shape=(state, state),
+        functools.partial(near_body, heads, not state, distance_of, deepest, n),
+        out_shape=(shape, shape),
         in_specs=[pl.BlockSpec(memory_space=pltpu.SMEM)]
-        + [pl.BlockSpec(memory_space=VMEM)] * 2
+        + [pl.BlockSpec(memory_space=VMEM)] * (2 + len(state))
         + [pl.BlockSpec(memory_space=pl.ANY)] * (2 * n),
         out_specs=(pl.BlockSpec(memory_space=VMEM),) * 2,
         scratch_shapes=[
@@ -272,11 +291,10 @@
             pltpu.SemaphoreType.DMA((2 * n,)),
         ],
         cost_estimate=pl.CostEstimate(
-            flops=16 * places * heads * rows * rows * HD, bytes_accessed=2 << 20, transcendentals=0
+            flops=4 * places * heads * rows * rows * HD, bytes_accessed=2 << 20, transcendentals=0
         ),
         compiler_params=pltpu.CompilerParams(vmem_limit_bytes=12 << 20),
-        name="attend_near",
-    )(span, queries, starts, *mine, *theirs)
+    )(span, queries, starts, *state, *mine, *theirs)
 
 
 def far_body(heads, n, span, queries, starts, total_in, weighted_in, *refs):
@@ -291,11 +309,13 @@
     for copy in copies:
         copy.wait()
 
+    deepest = LINE * LINE
+
     def distance_of(place):
-        return LINE - n + 1 + place // LINE + LINE * (place % LINE)
+        return LINE + LINE * place
 
     add_blocks(
-        heads, distance_of, kv.shape[1], span, queries, starts, kv, total, weighted, mask
+        heads, distance_of, deepest, span, queries, starts, kv, total, weighted, mask
     )
     for h in range(heads):
         sums = jnp.sum(total[h], axis=1, keepdims=True)
@@ -367,10 +387,22 @@
         hops.append(passed_along(hops[-1], 1))
         theirs = theirs + [swapped(hops[-2])]
     mine = [own] + hops
-    total, weighted = attend_near(span, queries, starts, mine[:3], theirs[:3])
     theirs.append(swapped(hops[-1]))
+    state = ()
+    for i, (low, high) in enumerate(((0, 2), (2, 3), (3, 4))):
+
+        def distance_of(place, i=i):
+            if i == 0:
+                return jnp.where(place == 0, 0, 1 + LINE * (place - 1))
+            return 1 + i + LINE * place
+
+        state = attend_near(
+            span, queries, starts, state, mine[low:high], theirs[low:high],
+            distance_of, 1 + i + LINE * (LINE - 1),
+        )
+    total, weighted = state
     keep, give = attend_far(
-        span, queries, starts, total, weighted, mine[3:], theirs[3:], w_out, chips
+        span, queries, starts, total, weighted, mine[4:], theirs[4:], w_out, chips
     )
     pairs = (keep.astype(jnp.float32) + swapped(give).astype(jnp.float32)).astype(jnp.bfloat16)
     terms = lax.all_to_all(pairs, "x", 0, 0, tiled=True)

time: 127 us -> 130 us (1.024)
  waiting for transfers between devices: 45.6 us -> 48.4 us
    pallas_call x1 -> x3, Pallas kernels: 6.91 us -> 9.76 us  [attend_near(): pl.pallas_call(functools.partial(near_body, heads, not state, distance_of...]
    ppermute x7, waiting for transfers between devices: 44.1 us -> 46.6 us  [passed_along(): lax.ppermute(a, 'ctx', [(i, i + distance) for i in range(n - distance)])]
    pallas_call x1, Pallas kernels: 4.75 us -> 2.88 us  [attend_far(): pl.pallas_call(functools.partial(far_body, heads, n), out_shape=(half, ha...]
  transfers between devices with their start and end apart: 13 -> 13, of which waited for: 6 -> 7; matrix products, arithmetic and copies ran while one was open for 0% -> 0% of each run, Pallas kernels for 9% -> 11%
where the time goes in v2:
time: 130 us
  waiting for transfers between devices  48.4 us (37%)
  starting transfers between devices  43.4 us (33%)
  Pallas kernels  20.8 us (16%)
  blocking collectives  13.9 us (11%)
  local copies, waits for them, and re-layouts  1.8 us (1%)
    ppermute x7, waiting for transfers between devices, passed_along(): lax.ppermute(a, 'ctx', [(i, i + distance) for i in range(n - distance)])  46.6 us
    ppermute x7, starting transfers between devices, passed_along(): lax.ppermute(a, 'ctx', [(i, i + distance) for i in range(n - distance)])  30.9 us
    all_to_all x1, blocking collectives, local(): terms = lax.all_to_all(pairs, 'x', 0, 0, tiled=True)  13.9 us
    ppermute x6, starting transfers between devices, swapped(): return lax.ppermute(a, 'c', [(0, 1), (1, 0)])  12.5 us
    pallas_call x3, Pallas kernels, attend_near(): pl.pallas_call(functools.partial(near_body, heads, not state, distance_of...  9.76 us
    pallas_call x1, Pallas kernels, project_q(): pl.pallas_call(q_body, out_shape=jax.ShapeDtypeStruct((heads, rows, HD),...  4.67 us
    pallas_call x1, Pallas kernels, project_kv(): pl.pallas_call(functools.partial(kv_body, heads), out_shape=(jax.ShapeDty...  3.5 us
    pallas_call x1, Pallas kernels, attend_far(): pl.pallas_call(functools.partial(far_body, heads, n), out_shape=(half, ha...  2.88 us
  transfers between devices with their start and end apart: 13, of which 7 were waited for; matrix products, arithmetic and copies ran while one was open for 0% of the time, Pallas kernels for 11%

profile of v2, /device:TPU:24, one launch (start us, length us, event | category | flops | bytes accessed | tf_op | source)
XLA Modules:
  0.0 129.5 jit_solution(9495532641671506542)
XLA Ops:
  0.0 3.5 %project_kv.1 = (bf16[256,128]{1,0:T(8,128)(2,1)}, f32[256,128]{1,0:T(8,128)}, f32[256,128]{1,0:T(8,128)}, s32[256,1]{1,0:T(8,128)}, s32[2]{0:T(128)}) custom-call(bf16[256,2048]{1,0:T(8,128)(2,1)} %tokens_hbm.3, bf16[2048,512]{1,0:T(8,128)(2,1)} %w_key.1, bf16[2048,512]{1,0:T(8,128)(2,1)} %w_value.1, f32[1,128]{1,0:T(1,128)} %bitcast.15, ...), custom_call_target="tpu_custom_call" | custom-call | flops 134217728 | bytes 2097152 | tf_op jit(solution)/shard_map/project_kv/pallas_call | solution.py:93
  3.5 10.5 %collective-permute-start.1 = (bf16[256,128]{1,0:T(8,128)(2,1)}, bf16[256,128]{1,0:T(8,128)(2,1)S(1)}, u32[]{:S(2)}, u32[]{:S(2)}) collective-permute-start(bf16[256,128]{1,0:T(8,128)(2,1)} %get-tuple-element.22), channel_id=1, source_target_pairs={{0,40},{8,48},{16,56},{24,64},{32,72},{40,80},{48,88},{56,96},{64,... | collective-permute-start | bytes 196616 | tf_op jit(solution)/shard_map/ppermute | solution.py:365
  14.0 13.9 %collective-permute-done.1 = bf16[256,128]{1,0:T(8,128)(2,1)S(1)} collective-permute-done((bf16[256,128]{1,0:T(8,128)(2,1)}, bf16[256,128]{1,0:T(8,128)(2,1)S(1)}, u32[]{:S(2)}, u32[]{:S(2)}) %collective-permute-start.1) | collective-permute-done | bytes 65568 | tf_op jit(solution)/shard_map/ppermute | solution.py:365
  27.9 9.5 %collective-permute-start.2 = (bf16[256,128]{1,0:T(8,128)(2,1)S(1)}, bf16[256,128]{1,0:T(8,128)(2,1)S(1)}, u32[]{:S(2)}, u32[]{:S(2)}) collective-permute-start(bf16[256,128]{1,0:T(8,128)(2,1)S(1)} %collective-permute-done.1), channel_id=1, source_target_pairs={{0,32},{8,40},{16,48},{24,56},{32,64},{40,72},{48,80},{56,88},{64,... | collective-permute-start | bytes 196616 | tf_op jit(solution)/shard_map/ppermute | solution.py:365
  37.4 1.9 %collective-permute-start = (bf16[256,128]{1,0:T(8,128)(2,1)}, bf16[256,128]{1,0:T(8,128)(2,1)S(1)}, u32[]{:S(2)}, u32[]{:S(2)}) collective-permute-start(bf16[256,128]{1,0:T(8,128)(2,1)} %get-tuple-element.22), channel_id=1, source_target_pairs={{0,8},{8,16},{16,24},{24,32},{32,40},{40,48},{48,56},{56,64},{64,7... | collective-permute-start | bytes 196616 | tf_op jit(solution)/shard_map/ppermute | solution.py:365
  39.3 5.2 %collective-permute-done.2 = bf16[256,128]{1,0:T(8,128)(2,1)S(1)} collective-permute-done((bf16[256,128]{1,0:T(8,128)(2,1)S(1)}, bf16[256,128]{1,0:T(8,128)(2,1)S(1)}, u32[]{:S(2)}, u32[]{:S(2)}) %collective-permute-start.2) | collective-permute-done | bytes 65568 | tf_op jit(solution)/shard_map/ppermute | solution.py:365
  44.5 3.0 %collective-permute-start.3 = (bf16[256,128]{1,0:T(8,128)(2,1)S(1)}, bf16[256,128]{1,0:T(8,128)(2,1)S(1)}, u32[]{:S(2)}, u32[]{:S(2)}) collective-permute-start(bf16[256,128]{1,0:T(8,128)(2,1)S(1)} %collective-permute-done.2), channel_id=1, source_target_pairs={{0,32},{8,40},{16,48},{24,56},{32,64},{40,72},{48,80},{56,88},{64,... | collective-permute-start | bytes 196616 | tf_op jit(solution)/shard_map/ppermute | solution.py:365
  47.4 0.0 collective-permute-done
  47.4 8.0 %collective-permute-done.3 = bf16[256,128]{1,0:T(8,128)(2,1)S(1)} collective-permute-done((bf16[256,128]{1,0:T(8,128)(2,1)S(1)}, bf16[256,128]{1,0:T(8,128)(2,1)S(1)}, u32[]{:S(2)}, u32[]{:S(2)}) %collective-permute-start.3) | collective-permute-done | bytes 65568 | tf_op jit(solution)/shard_map/ppermute | solution.py:365
  55.4 0.0 copy-start.3
  55.4 0.0 copy-start.4
  55.5 2.3 %collective-permute-start.6 = (bf16[4,256,128]{2,1,0:T(8,128)(2,1)S(1)}, bf16[4,256,128]{2,1,0:T(8,128)(2,1)}, u32[]{:S(2)}, u32[]{:S(2)}) collective-permute-start(bf16[4,256,128]{2,1,0:T(8,128)(2,1)S(1)} %pad_maximum_fusion.refs_1_), channel_id=1, source_target_pairs={{0,8},{8,16},{16,24},{24,32},{32,40},{40,48},{48,56},{56,64},{64,7... | collective-permute-start | bytes 786440 | tf_op jit(solution)/shard_map/ppermute | solution.py:365
  57.8 8.3 %collective-permute-done.6.refs_2_ = bf16[4,256,128]{2,1,0:T(8,128)(2,1)} collective-permute-done((bf16[4,256,128]{2,1,0:T(8,128)(2,1)S(1)}, bf16[4,256,128]{2,1,0:T(8,128)(2,1)}, u32[]{:S(2)}, u32[]{:S(2)}) %collective-permute-start.6) | collective-permute-done | bytes 262176 | tf_op jit(solution)/shard_map/ppermute | solution.py:365
  66.1 1.9 %collective-permute-start.8 = (bf16[4,256,128]{2,1,0:T(8,128)(2,1)}, bf16[4,256,128]{2,1,0:T(8,128)(2,1)}, u32[]{:S(2)}, u32[]{:S(2)}) collective-permute-start(bf16[4,256,128]{2,1,0:T(8,128)(2,1)} %collective-permute-done.6.refs_2_), channel_id=1, source_target_pairs={{0,8},{8,16},{16,24},{24,32},{32,40},{40,48},{48,56},{56,64},{64,7... | collective-permute-start | bytes 786440 | tf_op jit(solution)/shard_map/ppermute | solution.py:365
  68.0 8.8 %collective-permute-done.8.refs_2_ = bf16[4,256,128]{2,1,0:T(8,128)(2,1)} collective-permute-done((bf16[4,256,128]{2,1,0:T(8,128)(2,1)}, bf16[4,256,128]{2,1,0:T(8,128)(2,1)}, u32[]{:S(2)}, u32[]{:S(2)}) %collective-permute-start.8) | collective-permute-done | bytes 262176 | tf_op jit(solution)/shard_map/ppermute | solution.py:365
  76.8 1.9 %collective-permute-start.10 = (bf16[4,256,128]{2,1,0:T(8,128)(2,1)}, bf16[4,256,128]{2,1,0:T(8,128)(2,1)S(1)}, u32[]{:S(2)}, u32[]{:S(2)}) collective-permute-start(bf16[4,256,128]{2,1,0:T(8,128)(2,1)} %collective-permute-done.8.refs_2_), channel_id=1, source_target_pairs={{0,8},{8,16},{16,24},{24,32},{32,40},{40,48},{48,56},{56,64},{64,7... | collective-permute-start | bytes 786440 | tf_op jit(solution)/shard_map/ppermute | solution.py:365
  78.7 1.9 %collective-permute-start.5 = (bf16[4,256,128]{2,1,0:T(8,128)(2,1)S(1)}, bf16[4,256,128]{2,1,0:T(8,128)(2,1)}, u32[]{:S(2)}, u32[]{:S(2)}) collective-permute-start(bf16[4,256,128]{2,1,0:T(8,128)(2,1)S(1)} %pad_maximum_fusion.refs_1_), channel_id=1, source_target_pairs={{0,1},{1,0},{2,3},{3,2},{4,5},{5,4},{6,7},{7,6},{8,9},{9,8},{10,11... | collective-permute-start | bytes 786440 | tf_op jit(solution)/shard_map/ppermute | solution.py:369
  80.6 2.4 %collective-permute-start.7 = (bf16[4,256,128]{2,1,0:T(8,128)(2,1)}, bf16[4,256,128]{2,1,0:T(8,128)(2,1)}, u32[]{:S(2)}, u32[]{:S(2)}) collective-permute-start(bf16[4,256,128]{2,1,0:T(8,128)(2,1)} %collective-permute-done.6.refs_2_), channel_id=1, source_target_pairs={{0,1},{1,0},{2,3},{3,2},{4,5},{5,4},{6,7},{7,6},{8,9},{9,8},{10,11... | collective-permute-start | bytes 786440 | tf_op jit(solution)/shard_map/ppermute | solution.py:369
  83.0 1.9 %collective-permute-start.9 = (bf16[4,256,128]{2,1,0:T(8,128)(2,1)}, bf16[4,256,128]{2,1,0:T(8,128)(2,1)}, u32[]{:S(2)}, u32[]{:S(2)}) collective-permute-start(bf16[4,256,128]{2,1,0:T(8,128)(2,1)} %collective-permute-done.8.refs_2_), channel_id=1, source_target_pairs={{0,1},{1,0},{2,3},{3,2},{4,5},{5,4},{6,7},{7,6},{8,9},{9,8},{10,11... | collective-permute-start | bytes 786440 | tf_op jit(solution)/shard_map/ppermute | solution.py:369
  85.0 2.4 %collective-permute-done.10.refs_0_ = bf16[4,256,128]{2,1,0:T(8,128)(2,1)S(1)} collective-permute-done((bf16[4,256,128]{2,1,0:T(8,128)(2,1)}, bf16[4,256,128]{2,1,0:T(8,128)(2,1)S(1)}, u32[]{:S(2)}, u32[]{:S(2)}) %collective-permute-start.10) | collective-permute-done | bytes 262176 | tf_op jit(solution)/shard_map/ppermute | solution.py:365
  87.4 1.9 %collective-permute-start.11 = (bf16[4,256,128]{2,1,0:T(8,128)(2,1)S(1)}, bf16[4,256,128]{2,1,0:T(8,128)(2,1)S(1)}, u32[]{:S(2)}, u32[]{:S(2)}) collective-permute-start(bf16[4,256,128]{2,1,0:T(8,128)(2,1)S(1)} %collective-permute-done.10.refs_0_), channel_id=1, source_target_pairs={{0,1},{1,0},{2,3},{3,2},{4,5},{5,4},{6,7},{7,6},{8,9},{9,8},{10,11... | collective-permute-start | bytes 786440 | tf_op jit(solution)/shard_map/ppermute | solution.py:369
  89.3 2.4 %collective-permute-start.4 = (bf16[1,256,128]{2,1,0:T(8,128)(2,1)}, bf16[1,256,128]{2,1,0:T(8,128)(2,1)}, u32[]{:S(2)}, u32[]{:S(2)}) collective-permute-start(bf16[1,256,128]{2,1,0:T(8,128)(2,1)} %bitcast.8), channel_id=1, source_target_pairs={{0,1},{1,0},{2,3},{3,2},{4,5},{5,4},{6,7},{7,6},{8,9},{9,8},{10,11... | collective-permute-start | bytes 196616 | tf_op jit(solution)/shard_map/ppermute | solution.py:369
  91.7 4.7 %project_q.1.queries = bf16[4,256,128]{2,1,0:T(8,128)(2,1)} custom-call(bf16[256,2048]{1,0:T(8,128)(2,1)} %tokens_hbm.3, bf16[2048,512]{1,0:T(8,128)(2,1)} %w_hbm.1, f32[1,128]{1,0:T(1,128)} %bitcast.16, f32[256,128]{1,0:T(8,128)} %get-tuple-element.19.cosine_any, f32[256,128]{1,0:T(8,128)} %get-tuple-element.20.sine_any), custom_call_target="tpu_custom_call" | custom-call | flops 536870912 | bytes 3145728 | tf_op jit(solution)/shard_map/project_q/pallas_call | solution.py:153
  96.4 0.0 collective-permute-done.4.refs_2_
  96.4 0.0 collective-permute-done.5.refs_3_
  96.4 0.0 copy-done.3
  96.4 0.0 copy-done.4
  96.4 0.0 copy-start.1
  96.4 0.9 copy-done.1
  97.4 0.0 copy-start.5
  97.4 0.8 copy-done.5
  98.2 0.0 copy-start.2
  98.2 3.8 %shard_map.91 = (f32[4,256,128]{2,1,0:T(8,128)S(1)}, f32[4,256,128]{2,1,0:T(8,128)S(1)}) custom-call(s32[2]{0:T(128)S(1)} %copy-done.4, bf16[4,256,128]{2,1,0:T(8,128)(2,1)S(1)} %copy-done.1, s32[256,1]{1,0:T(8,128)S(1)} %copy-done.3, bf16[1,256,128]{2,1,0:T(8,128)(2,1)S(1)} %bitcast.9, bf16[4,256,128]{2,1,0:T(8,128)(2,1)S(1)} %pad_maximum_fusion.refs_1_, ...), custom_call_target="tpu_custom_call" | custom-call | flops 671088640 | bytes 2097152 | tf_op jit(solution)/shard_map/pallas_call | solution.py:281
  102.0 0.0 copy-start
  102.0 0.0 collective-permute-done.7.refs_3_
  102.1 0.0 copy-done.2
  102.1 3.3 %shard_map.92 = (f32[4,256,128]{2,1,0:T(8,128)S(1)}, f32[4,256,128]{2,1,0:T(8,128)S(1)}) custom-call(s32[2]{0:T(128)S(1)} %copy-done.4, bf16[4,256,128]{2,1,0:T(8,128)(2,1)S(1)} %copy-done.2, s32[256,1]{1,0:T(8,128)S(1)} %copy-done.3, f32[4,256,128]{2,1,0:T(8,128)S(1)} %get-tuple-element.23.refs_0_, f32[4,256,128]{2,1,0:T(8,128)S(1)} %get-tuple-element.24.refs_1_, ...), custom_call_target="tpu_custom_call" | custom-call | flops 536870912 | bytes 2097152 | tf_op jit(solution)/shard_map/pallas_call | solution.py:281
  105.3 0.0 collective-permute-done.9.refs_3_
  105.3 2.7 %shard_map.93 = (f32[4,256,128]{2,1,0:T(8,128)S(1)}, f32[4,256,128]{2,1,0:T(8,128)S(1)}) custom-call(s32[2]{0:T(128)S(1)} %copy-done.4, bf16[4,256,128]{2,1,0:T(8,128)(2,1)S(1)} %copy-done.2, s32[256,1]{1,0:T(8,128)S(1)} %copy-done.3, f32[4,256,128]{2,1,0:T(8,128)S(1)} %get-tuple-element.25.refs_0_, f32[4,256,128]{2,1,0:T(8,128)S(1)} %get-tuple-element.26.refs_1_, ...), custom_call_target="tpu_custom_call" | custom-call | flops 536870912 | bytes 2097152 | tf_op jit(solution)/shard_map/pallas_call | solution.py:281
  108.0 0.0 collective-permute-done.11.refs_1_
  108.0 0.0 copy-done
  108.1 2.9 %attend_far.1 = (bf16[4,256,256]{2,1,0:T(8,128)(2,1)S(1)}, bf16[4,256,256]{2,1,0:T(8,128)(2,1)S(1)}) custom-call(s32[2]{0:T(128)S(1)} %copy-done.4, bf16[4,256,128]{2,1,0:T(8,128)(2,1)S(1)} %copy-done.2, s32[256,1]{1,0:T(8,128)S(1)} %copy-done.3, f32[4,256,128]{2,1,0:T(8,128)S(1)} %get-tuple-element.27.total_in, ...), custom_call_target="tpu_custom_call" | custom-call | flops 536870912 | bytes 4194304 | tf_op jit(solution)/shard_map/attend_far/pallas_call | solution.py:339
  110.9 1.9 %collective-permute-start.12 = (bf16[4,256,256]{2,1,0:T(8,128)(2,1)S(1)}, bf16[4,256,256]{2,1,0:T(8,128)(2,1)S(1)}, u32[]{:S(2)}, u32[]{:S(2)}) collective-permute-start(bf16[4,256,256]{2,1,0:T(8,128)(2,1)S(1)} %get-tuple-element.30), channel_id=1, source_target_pairs={{0,1},{1,0},{2,3},{3,2},{4,5},{5,4},{6,7},{7,6},{8,9},{9,8},{10,11... | collective-permute-start | bytes 1572872 | tf_op jit(solution)/shard_map/ppermute | solution.py:369
  112.9 1.9 %collective-permute-done.12 = bf16[4,256,256]{2,1,0:T(8,128)(2,1)S(1)} collective-permute-done((bf16[4,256,256]{2,1,0:T(8,128)(2,1)S(1)}, bf16[4,256,256]{2,1,0:T(8,128)(2,1)S(1)}, u32[]{:S(2)}, u32[]{:S(2)}) %collective-permute-start.12) | collective-permute-done | bytes 524320 | tf_op jit(solution)/shard_map/ppermute | solution.py:369
  114.7 0.1 add_convert_fusion
  114.9 13.9 %all_to_all.5 = bf16[4,256,256]{2,1,0:T(8,128)(2,1)S(1)} all-to-all(bf16[4,256,256]{2,1,0:T(8,128)(2,1)S(1)} %add_convert_fusion), channel_id=1, replica_groups=mesh['ctx'=128,'x'=4,'c'=2] {'x'}, dimensions={0} | all-to-all | bytes 1048576 | tf_op jit(solution)/shard_map/all_to_all | solution.py:408
  128.8 0.7 reduce_sum.12
  (1 shorter events, 0.0 us)
Async XLA Ops:
  3.5 24.4 %collective-permute-start.1 = (bf16[256,128]{1,0:T(8,128)(2,1)}, bf16[256,128]{1,0:T(8,128)(2,1)S(1)}, u32[]{:S(2)}, u32[]{:S(2)}) collective-permute-start(bf16[256,128]{1,0:T(8,128)(2,1)} %get-tuple-element.22), channel_id=1, source_target_pairs={{0,40},{8,48},{16,56},{24,64},{32,72},{40,80},{48,88},{56,96},{64,... | collective-permute-start | bytes 196616 | tf_op jit(solution)/shard_map/ppermute | solution.py:365
  27.9 16.5 %collective-permute-start.2 = (bf16[256,128]{1,0:T(8,128)(2,1)S(1)}, bf16[256,128]{1,0:T(8,128)(2,1)S(1)}, u32[]{:S(2)}, u32[]{:S(2)}) collective-permute-start(bf16[256,128]{1,0:T(8,128)(2,1)S(1)} %collective-permute-done.1), channel_id=1, source_target_pairs={{0,32},{8,40},{16,48},{24,56},{32,64},{40,72},{48,80},{56,88},{64,... | collective-permute-start | bytes 196616 | tf_op jit(solution)/shard_map/ppermute | solution.py:365
  37.4 10.1 %collective-permute-start = (bf16[256,128]{1,0:T(8,128)(2,1)}, bf16[256,128]{1,0:T(8,128)(2,1)S(1)}, u32[]{:S(2)}, u32[]{:S(2)}) collective-permute-start(bf16[256,128]{1,0:T(8,128)(2,1)} %get-tuple-element.22), channel_id=1, source_target_pairs={{0,8},{8,16},{16,24},{24,32},{32,40},{40,48},{48,56},{56,64},{64,7... | collective-permute-start | bytes 196616 | tf_op jit(solution)/shard_map/ppermute | solution.py:365
  44.5 11.0 %collective-permute-start.3 = (bf16[256,128]{1,0:T(8,128)(2,1)S(1)}, bf16[256,128]{1,0:T(8,128)(2,1)S(1)}, u32[]{:S(2)}, u32[]{:S(2)}) collective-permute-start(bf16[256,128]{1,0:T(8,128)(2,1)S(1)} %collective-permute-done.2), channel_id=1, source_target_pairs={{0,32},{8,40},{16,48},{24,56},{32,64},{40,72},{48,80},{56,88},{64,... | collective-permute-start | bytes 196616 | tf_op jit(solution)/shard_map/ppermute | solution.py:365
  55.4 41.0 %copy-start.3 = (s32[256,1]{1,0:T(8,128)S(1)}, s32[256,1]{1,0:T(8,128)}, u32[]{:S(2)}) copy-start(s32[256,1]{1,0:T(8,128)} %get-tuple-element.21.starts) | copy-start | bytes 3076
  55.4 41.0 %copy-start.4 = (s32[2]{0:T(128)S(1)}, s32[2]{0:T(128)}, u32[]{:S(2)}) copy-start(s32[2]{0:T(128)} %get-tuple-element.18.span) | copy-start | bytes 28
  55.5 10.6 %collective-permute-start.6 = (bf16[4,256,128]{2,1,0:T(8,128)(2,1)S(1)}, bf16[4,256,128]{2,1,0:T(8,128)(2,1)}, u32[]{:S(2)}, u32[]{:S(2)}) collective-permute-start(bf16[4,256,128]{2,1,0:T(8,128)(2,1)S(1)} %pad_maximum_fusion.refs_1_), channel_id=1, source_target_pairs={{0,8},{8,16},{16,24},{24,32},{32,40},{40,48},{48,56},{56,64},{64,7... | collective-permute-start | bytes 786440 | tf_op jit(solution)/shard_map/ppermute | solution.py:365
  66.1 10.7 %collective-permute-start.8 = (bf16[4,256,128]{2,1,0:T(8,128)(2,1)}, bf16[4,256,128]{2,1,0:T(8,128)(2,1)}, u32[]{:S(2)}, u32[]{:S(2)}) collective-permute-start(bf16[4,256,128]{2,1,0:T(8,128)(2,1)} %collective-permute-done.6.refs_2_), channel_id=1, source_target_pairs={{0,8},{8,16},{16,24},{24,32},{32,40},{40,48},{48,56},{56,64},{64,7... | collective-permute-start | bytes 786440 | tf_op jit(solution)/shard_map/ppermute | solution.py:365
  76.8 10.6 %collective-permute-start.10 = (bf16[4,256,128]{2,1,0:T(8,128)(2,1)}, bf16[4,256,128]{2,1,0:T(8,128)(2,1)S(1)}, u32[]{:S(2)}, u32[]{:S(2)}) collective-permute-start(bf16[4,256,128]{2,1,0:T(8,128)(2,1)} %collective-permute-done.8.refs_2_), channel_id=1, source_target_pairs={{0,8},{8,16},{16,24},{24,32},{32,40},{40,48},{48,56},{56,64},{64,7... | collective-permute-start | bytes 786440 | tf_op jit(solution)/shard_map/ppermute | solution.py:365
  78.7 17.7 %collective-permute-start.5 = (bf16[4,256,128]{2,1,0:T(8,128)(2,1)S(1)}, bf16[4,256,128]{2,1,0:T(8,128)(2,1)}, u32[]{:S(2)}, u32[]{:S(2)}) collective-permute-start(bf16[4,256,128]{2,1,0:T(8,128)(2,1)S(1)} %pad_maximum_fusion.refs_1_), channel_id=1, source_target_pairs={{0,1},{1,0},{2,3},{3,2},{4,5},{5,4},{6,7},{7,6},{8,9},{9,8},{10,11... | collective-permute-start | bytes 786440 | tf_op jit(solution)/shard_map/ppermute | solution.py:369
  80.6 21.4 %collective-permute-start.7 = (bf16[4,256,128]{2,1,0:T(8,128)(2,1)}, bf16[4,256,128]{2,1,0:T(8,128)(2,1)}, u32[]{:S(2)}, u32[]{:S(2)}) collective-permute-start(bf16[4,256,128]{2,1,0:T(8,128)(2,1)} %collective-permute-done.6.refs_2_), channel_id=1, source_target_pairs={{0,1},{1,0},{2,3},{3,2},{4,5},{5,4},{6,7},{7,6},{8,9},{9,8},{10,11... | collective-permute-start | bytes 786440 | tf_op jit(solution)/shard_map/ppermute | solution.py:369
  83.0 22.3 %collective-permute-start.9 = (bf16[4,256,128]{2,1,0:T(8,128)(2,1)}, bf16[4,256,128]{2,1,0:T(8,128)(2,1)}, u32[]{:S(2)}, u32[]{:S(2)}) collective-permute-start(bf16[4,256,128]{2,1,0:T(8,128)(2,1)} %collective-permute-done.8.refs_2_), channel_id=1, source_target_pairs={{0,1},{1,0},{2,3},{3,2},{4,5},{5,4},{6,7},{7,6},{8,9},{9,8},{10,11... | collective-permute-start | bytes 786440 | tf_op jit(solution)/shard_map/ppermute | solution.py:369
  87.4 20.7 %collective-permute-start.11 = (bf16[4,256,128]{2,1,0:T(8,128)(2,1)S(1)}, bf16[4,256,128]{2,1,0:T(8,128)(2,1)S(1)}, u32[]{:S(2)}, u32[]{:S(2)}) collective-permute-start(bf16[4,256,128]{2,1,0:T(8,128)(2,1)S(1)} %collective-permute-done.10.refs_0_), channel_id=1, source_target_pairs={{0,1},{1,0},{2,3},{3,2},{4,5},{5,4},{6,7},{7,6},{8,9},{9,8},{10,11... | collective-permute-start | bytes 786440 | tf_op jit(solution)/shard_map/ppermute | solution.py:369
  89.3 7.1 %collective-permute-start.4 = (bf16[1,256,128]{2,1,0:T(8,128)(2,1)}, bf16[1,256,128]{2,1,0:T(8,128)(2,1)}, u32[]{:S(2)}, u32[]{:S(2)}) collective-permute-start(bf16[1,256,128]{2,1,0:T(8,128)(2,1)} %bitcast.8), channel_id=1, source_target_pairs={{0,1},{1,0},{2,3},{3,2},{4,5},{5,4},{6,7},{7,6},{8,9},{9,8},{10,11... | collective-permute-start | bytes 196616 | tf_op jit(solution)/shard_map/ppermute | solution.py:369
  96.4 1.0 copy-start.1
  97.4 0.8 copy-start.5
  98.2 3.9 %copy-start.2 = (bf16[4,256,128]{2,1,0:T(8,128)(2,1)S(1)}, bf16[4,256,128]{2,1,0:T(8,128)(2,1)}, u32[]{:S(2)}) copy-start(bf16[4,256,128]{2,1,0:T(8,128)(2,1)} %project_q.1.queries) | copy-start | bytes 786436
  102.0 6.0 %copy-start = (bf16[512,2048]{1,0:T(8,128)(2,1)S(1)}, bf16[512,2048]{1,0:T(8,128)(2,1)}, u32[]{:S(2)}) copy-start(bf16[512,2048]{1,0:T(8,128)(2,1)} %refs_2_.1) | copy-start | bytes 6291460
  110.9 3.8 %collective-permute-start.12 = (bf16[4,256,256]{2,1,0:T(8,128)(2,1)S(1)}, bf16[4,256,256]{2,1,0:T(8,128)(2,1)S(1)}, u32[]{:S(2)}, u32[]{:S(2)}) collective-permute-start(bf16[4,256,256]{2,1,0:T(8,128)(2,1)S(1)} %get-tuple-element.30), channel_id=1, source_target_pairs={{0,1},{1,0},{2,3},{3,2},{4,5},{5,4},{6,7},{7,6},{8,9},{9,8},{10,11... | collective-permute-start | bytes 1572872 | tf_op jit(solution)/shard_map/ppermute | solution.py:369

commit v3 on v2

--- a/solution.py
+++ b/solution.py
@@ -12,6 +12,7 @@
 H = 32
 KVH = 4
 HD = 128
+REACH = 16
 LINE = 4
 EPSILON = 1e-06
 ROPE_BASE = 1000000.0
@@ -224,14 +225,16 @@
 
         return carry
 
-    together = (block - deepest) * rows >= last
-
-    @pl.when(together)
-    def _():
-        four = pl.ds(places - LINE, LINE)
-        key = kv[0, four].reshape(LINE * rows, HD)
-        value = kv[1, four].reshape(LINE * rows, HD)
-        add_block(heads, queries, key, value, total, weighted, None)
+    together = (places == LINE) & ((block - deepest) * rows >= last) & (deepest > 0)
+
+    if places == LINE:
+
+        @pl.when(together)
+        def _():
+            four = pl.ds(places - LINE, LINE)
+            key = kv[0, four].reshape(LINE * rows, HD)
+            value = kv[1, four].reshape(LINE * rows, HD)
+            add_block(heads, queries, key, value, total, weighted, None)
 
     lax.fori_loop(0, jnp.where(together, places - LINE, places), step, 0)
 
@@ -309,10 +312,10 @@
     for copy in copies:
         copy.wait()
 
-    deepest = LINE * LINE
+    deepest = 0
 
     def distance_of(place):
-        return LINE + LINE * place
+        return REACH + place
 
     add_blocks(
         heads, distance_of, deepest, span, queries, starts, kv, total, weighted, mask
@@ -382,27 +385,31 @@
     for _ in range(2):
         far.append(passed_along(far[-1], LINE))
     queries = project_q(tokens, w_query, query_gain[None], cosine, sine)
-    hops = [jnp.stack([near] + far)]
-    for _ in range(LINE - 1):
-        hops.append(passed_along(hops[-1], 1))
+    early = jnp.stack([near] + far[:2])
+    moved = passed_along(early, 1)
+    theirs.append(swapped(early))
+    hops = [jnp.concatenate([moved, far[2][None]])]
+    for i in range(LINE - 1):
+        moving = hops[-1] if i < LINE - 2 else hops[-1][LINE - 1 :]
+        hops.append(passed_along(moving, 1))
         theirs = theirs + [swapped(hops[-2])]
-    mine = [own] + hops
+    mine = [own, early] + hops
     theirs.append(swapped(hops[-1]))
     state = ()
-    for i, (low, high) in enumerate(((0, 2), (2, 3), (3, 4))):
+    for i, (low, high) in enumerate(((0, 2), (2, 3), (3, 4), (4, 5))):
 
         def distance_of(place, i=i):
             if i == 0:
                 return jnp.where(place == 0, 0, 1 + LINE * (place - 1))
-            return 1 + i + LINE * place
+            return jnp.where(place == LINE - 1, 12 + i, 1 + i + LINE * place)
 
         state = attend_near(
             span, queries, starts, state, mine[low:high], theirs[low:high],
-            distance_of, 1 + i + LINE * (LINE - 1),
+            distance_of, 12 + i if i else 0,
         )
     total, weighted = state
     keep, give = attend_far(
-        span, queries, starts, total, weighted, mine[4:], theirs[4:], w_out, chips
+        span, queries, starts, total, weighted, mine[5:], theirs[5:], w_out, chips
     )
     pairs = (keep.astype(jnp.float32) + swapped(give).astype(jnp.float32)).astype(jnp.bfloat16)
     terms = lax.all_to_all(pairs, "x", 0, 0, tiled=True)

time: 130 us -> 129 us (level)
  waiting for transfers between devices: 48.4 us -> 36.4 us
  starting transfers between devices: 43.4 us -> 51.9 us
  Pallas kernels: 20.8 us -> 22.7 us
    ppermute x7 -> x8, waiting for transfers between devices: 46.6 us -> 34.8 us  [passed_along(): lax.ppermute(a, 'ctx', [(i, i + distance) for i in range(n - distance)])]
    ppermute x7 -> x8, starting transfers between devices: 30.9 us -> 36.9 us  [passed_along(): lax.ppermute(a, 'ctx', [(i, i + distance) for i in range(n - distance)])]
    pallas_call x3 -> x4, Pallas kernels: 9.76 us -> 12.6 us  [attend_near(): pl.pallas_call(functools.partial(near_body, heads, not state, distance_of...]
    ppermute x6 -> x7, starting transfers between devices: 12.5 us -> 15 us  [swapped(): return lax.ppermute(a, 'c', [(0, 1), (1, 0)])]
  transfers between devices with their start and end apart: 13 -> 15, of which waited for: 7 -> 6; matrix products, arithmetic and copies ran while one was open for 0% -> 0% of each run, Pallas kernels for 11% -> 13%
where the time goes in v3:
time: 129 us; the launch traced here: 128 us
  starting transfers between devices  51.9 us (40%)
  waiting for transfers between devices  36.4 us (28%)
  Pallas kernels  22.7 us (18%)
  blocking collectives  14.1 us (11%)
  local copies, waits for them, and re-layouts  1.91 us (1%)
    ppermute x8, starting transfers between devices, passed_along(): lax.ppermute(a, 'ctx', [(i, i + distance) for i in range(n - distance)])  36.9 us
    ppermute x8, waiting for transfers between devices, passed_along(): lax.ppermute(a, 'ctx', [(i, i + distance) for i in range(n - distance)])  34.8 us
    ppermute x7, starting transfers between devices, swapped(): return lax.ppermute(a, 'c', [(0, 1), (1, 0)])  15 us
    all_to_all x1, blocking collectives, local(): terms = lax.all_to_all(pairs, 'x', 0, 0, tiled=True)  14.1 us
    pallas_call x4, Pallas kernels, attend_near(): pl.pallas_call(functools.partial(near_body, heads, not state, distance_of...  12.6 us
    pallas_call x1, Pallas kernels, project_q(): pl.pallas_call(q_body, out_shape=jax.ShapeDtypeStruct((heads, rows, HD),...  4.67 us
    pallas_call x1, Pallas kernels, project_kv(): pl.pallas_call(functools.partial(kv_body, heads), out_shape=(jax.ShapeDty...  3.5 us
  transfers between devices with their start and end apart: 15, of which 6 were waited for; matrix products, arithmetic and copies ran while one was open for 0% of the time, Pallas kernels for 13%

profile of v3, /device:TPU:24, one launch (start us, length us, event | category | flops | bytes accessed | tf_op | source)
XLA Modules:
  0.0 128.3 jit_solution(202175511455944794)
XLA Ops:
  0.0 3.5 %project_kv.1 = (bf16[256,128]{1,0:T(8,128)(2,1)}, f32[256,128]{1,0:T(8,128)}, f32[256,128]{1,0:T(8,128)}, s32[256,1]{1,0:T(8,128)}, s32[2]{0:T(128)}) custom-call(bf16[256,2048]{1,0:T(8,128)(2,1)} %tokens_hbm.3, bf16[2048,512]{1,0:T(8,128)(2,1)} %w_key.1, bf16[2048,512]{1,0:T(8,128)(2,1)} %w_value.1, f32[1,128]{1,0:T(1,128)} %bitcast.15, ...), custom_call_target="tpu_custom_call" | custom-call | flops 134217728 | bytes 2097152 | tf_op jit(solution)/shard_map/project_kv/pallas_call | solution.py:94
  3.5 10.5 %collective-permute-start.1 = (bf16[256,128]{1,0:T(8,128)(2,1)}, bf16[256,128]{1,0:T(8,128)(2,1)S(1)}, u32[]{:S(2)}, u32[]{:S(2)}) collective-permute-start(bf16[256,128]{1,0:T(8,128)(2,1)} %get-tuple-element.24), channel_id=1, source_target_pairs={{0,40},{8,48},{16,56},{24,64},{32,72},{40,80},{48,88},{56,96},{64,... | collective-permute-start | bytes 196616 | tf_op jit(solution)/shard_map/ppermute | solution.py:368
  14.0 3.8 %collective-permute-start = (bf16[256,128]{1,0:T(8,128)(2,1)}, bf16[256,128]{1,0:T(8,128)(2,1)S(1)}, u32[]{:S(2)}, u32[]{:S(2)}) collective-permute-start(bf16[256,128]{1,0:T(8,128)(2,1)} %get-tuple-element.24), channel_id=1, source_target_pairs={{0,8},{8,16},{16,24},{24,32},{32,40},{40,48},{48,56},{56,64},{64,7... | collective-permute-start | bytes 196616 | tf_op jit(solution)/shard_map/ppermute | solution.py:368
  17.8 10.1 %collective-permute-done.1 = bf16[256,128]{1,0:T(8,128)(2,1)S(1)} collective-permute-done((bf16[256,128]{1,0:T(8,128)(2,1)}, bf16[256,128]{1,0:T(8,128)(2,1)S(1)}, u32[]{:S(2)}, u32[]{:S(2)}) %collective-permute-start.1) | collective-permute-done | bytes 65568 | tf_op jit(solution)/shard_map/ppermute | solution.py:368
  27.9 10.0 %collective-permute-start.2 = (bf16[256,128]{1,0:T(8,128)(2,1)S(1)}, bf16[256,128]{1,0:T(8,128)(2,1)S(1)}, u32[]{:S(2)}, u32[]{:S(2)}) collective-permute-start(bf16[256,128]{1,0:T(8,128)(2,1)S(1)} %collective-permute-done.1), channel_id=1, source_target_pairs={{0,32},{8,40},{16,48},{24,56},{32,64},{40,72},{48,80},{56,88},{64,... | collective-permute-start | bytes 196616 | tf_op jit(solution)/shard_map/ppermute | solution.py:368
  37.9 0.0 collective-permute-done
  37.9 5.3 %collective-permute-done.2 = bf16[256,128]{1,0:T(8,128)(2,1)S(1)} collective-permute-done((bf16[256,128]{1,0:T(8,128)(2,1)S(1)}, bf16[256,128]{1,0:T(8,128)(2,1)S(1)}, u32[]{:S(2)}, u32[]{:S(2)}) %collective-permute-start.2) | collective-permute-done | bytes 65568 | tf_op jit(solution)/shard_map/ppermute | solution.py:368
  43.2 2.0 %collective-permute-start.5 = (bf16[3,256,128]{2,1,0:T(8,128)(2,1)S(1)}, bf16[3,256,128]{2,1,0:T(8,128)(2,1)S(1)}, u32[]{:S(2)}, u32[]{:S(2)}) collective-permute-start(bf16[3,256,128]{2,1,0:T(8,128)(2,1)S(1)} %pad_maximum_fusion.1.refs_1_), channel_id=1, source_target_pairs={{0,8},{8,16},{16,24},{24,32},{32,40},{40,48},{48,56},{56,64},{64,7... | collective-permute-start | bytes 589832 | tf_op jit(solution)/shard_map/ppermute | solution.py:368
  45.2 4.7 %collective-permute-start.6 = (bf16[256,128]{1,0:T(8,128)(2,1)S(1)}, bf16[256,128]{1,0:T(8,128)(2,1)S(1)}, u32[]{:S(2)}, u32[]{:S(2)}) collective-permute-start(bf16[256,128]{1,0:T(8,128)(2,1)S(1)} %collective-permute-done.2), channel_id=1, source_target_pairs={{0,32},{8,40},{16,48},{24,56},{32,64},{40,72},{48,80},{56,88},{64,... | collective-permute-start | bytes 196616 | tf_op jit(solution)/shard_map/ppermute | solution.py:368
  49.9 8.0 %collective-permute-done.6 = bf16[256,128]{1,0:T(8,128)(2,1)S(1)} collective-permute-done((bf16[256,128]{1,0:T(8,128)(2,1)S(1)}, bf16[256,128]{1,0:T(8,128)(2,1)S(1)}, u32[]{:S(2)}, u32[]{:S(2)}) %collective-permute-start.6) | collective-permute-done | bytes 65568 | tf_op jit(solution)/shard_map/ppermute | solution.py:368
  58.0 0.0 collective-permute-done.5
  58.0 0.0 copy-start.4
  58.0 0.0 copy-start.5
  58.0 0.0 copy-start.6
  58.0 2.1 %collective-permute-start.8 = (bf16[4,256,128]{2,1,0:T(8,128)(2,1)S(1)}, bf16[4,256,128]{2,1,0:T(8,128)(2,1)}, u32[]{:S(2)}, u32[]{:S(2)}) collective-permute-start(bf16[4,256,128]{2,1,0:T(8,128)(2,1)S(1)} %pad_maximum_fusion.refs_2_), channel_id=1, source_target_pairs={{0,8},{8,16},{16,24},{24,32},{32,40},{40,48},{48,56},{56,64},{64,7... | collective-permute-start | bytes 786440 | tf_op jit(solution)/shard_map/ppermute | solution.py:368
  60.1 8.9 %collective-permute-done.8.refs_2_ = bf16[4,256,128]{2,1,0:T(8,128)(2,1)} collective-permute-done((bf16[4,256,128]{2,1,0:T(8,128)(2,1)S(1)}, bf16[4,256,128]{2,1,0:T(8,128)(2,1)}, u32[]{:S(2)}, u32[]{:S(2)}) %collective-permute-start.8) | collective-permute-done | bytes 262176 | tf_op jit(solution)/shard_map/ppermute | solution.py:368
  69.0 1.9 %collective-permute-start.10 = (bf16[4,256,128]{2,1,0:T(8,128)(2,1)}, bf16[4,256,128]{2,1,0:T(8,128)(2,1)S(1)}, u32[]{:S(2)}, u32[]{:S(2)}) collective-permute-start(bf16[4,256,128]{2,1,0:T(8,128)(2,1)} %collective-permute-done.8.refs_2_), channel_id=1, source_target_pairs={{0,8},{8,16},{16,24},{24,32},{32,40},{40,48},{48,56},{56,64},{64,7... | collective-permute-start | bytes 786440 | tf_op jit(solution)/shard_map/ppermute | solution.py:368
  70.9 1.9 %collective-permute-start.7 = (bf16[4,256,128]{2,1,0:T(8,128)(2,1)S(1)}, bf16[4,256,128]{2,1,0:T(8,128)(2,1)}, u32[]{:S(2)}, u32[]{:S(2)}) collective-permute-start(bf16[4,256,128]{2,1,0:T(8,128)(2,1)S(1)} %pad_maximum_fusion.refs_2_), channel_id=1, source_target_pairs={{0,1},{1,0},{2,3},{3,2},{4,5},{5,4},{6,7},{7,6},{8,9},{9,8},{10,11... | collective-permute-start | bytes 786440 | tf_op jit(solution)/shard_map/ppermute | solution.py:372
  72.9 2.4 %collective-permute-start.4 = (bf16[3,256,128]{2,1,0:T(8,128)(2,1)S(1)}, bf16[3,256,128]{2,1,0:T(8,128)(2,1)}, u32[]{:S(2)}, u32[]{:S(2)}) collective-permute-start(bf16[3,256,128]{2,1,0:T(8,128)(2,1)S(1)} %pad_maximum_fusion.1.refs_1_), channel_id=1, source_target_pairs={{0,1},{1,0},{2,3},{3,2},{4,5},{5,4},{6,7},{7,6},{8,9},{9,8},{10,11... | collective-permute-start | bytes 589832 | tf_op jit(solution)/shard_map/ppermute | solution.py:372
  75.3 1.9 %collective-permute-start.9 = (bf16[4,256,128]{2,1,0:T(8,128)(2,1)}, bf16[4,256,128]{2,1,0:T(8,128)(2,1)}, u32[]{:S(2)}, u32[]{:S(2)}) collective-permute-start(bf16[4,256,128]{2,1,0:T(8,128)(2,1)} %collective-permute-done.8.refs_2_), channel_id=1, source_target_pairs={{0,1},{1,0},{2,3},{3,2},{4,5},{5,4},{6,7},{7,6},{8,9},{9,8},{10,11... | collective-permute-start | bytes 786440 | tf_op jit(solution)/shard_map/ppermute | solution.py:372
  77.2 2.5 %collective-permute-done.10.refs_2_ = bf16[4,256,128]{2,1,0:T(8,128)(2,1)S(1)} collective-permute-done((bf16[4,256,128]{2,1,0:T(8,128)(2,1)}, bf16[4,256,128]{2,1,0:T(8,128)(2,1)S(1)}, u32[]{:S(2)}, u32[]{:S(2)}) %collective-permute-start.10) | collective-permute-done | bytes 262176 | tf_op jit(solution)/shard_map/ppermute | solution.py:368
  79.7 1.9 %collective-permute-start.11 = (bf16[4,256,128]{2,1,0:T(8,128)(2,1)S(1)}, bf16[4,256,128]{2,1,0:T(8,128)(2,1)}, u32[]{:S(2)}, u32[]{:S(2)}) collective-permute-start(bf16[4,256,128]{2,1,0:T(8,128)(2,1)S(1)} %collective-permute-done.10.refs_2_), channel_id=1, source_target_pairs={{0,1},{1,0},{2,3},{3,2},{4,5},{5,4},{6,7},{7,6},{8,9},{9,8},{10,11... | collective-permute-start | bytes 786440 | tf_op jit(solution)/shard_map/ppermute | solution.py:372
  81.7 2.4 %collective-permute-start.3 = (bf16[1,256,128]{2,1,0:T(8,128)(2,1)}, bf16[1,256,128]{2,1,0:T(8,128)(2,1)}, u32[]{:S(2)}, u32[]{:S(2)}) collective-permute-start(bf16[1,256,128]{2,1,0:T(8,128)(2,1)} %bitcast.8), channel_id=1, source_target_pairs={{0,1},{1,0},{2,3},{3,2},{4,5},{5,4},{6,7},{7,6},{8,9},{9,8},{10,11... | collective-permute-start | bytes 196616 | tf_op jit(solution)/shard_map/ppermute | solution.py:372
  84.1 4.7 %project_q.1.queries = bf16[4,256,128]{2,1,0:T(8,128)(2,1)} custom-call(bf16[256,2048]{1,0:T(8,128)(2,1)} %tokens_hbm.3, bf16[2048,512]{1,0:T(8,128)(2,1)} %w_hbm.1, f32[1,128]{1,0:T(1,128)} %bitcast.16, f32[256,128]{1,0:T(8,128)} %get-tuple-element.21.cosine_any, f32[256,128]{1,0:T(8,128)} %get-tuple-element.22.sine_any), custom_call_target="tpu_custom_call" | custom-call | flops 536870912 | bytes 3145728 | tf_op jit(solution)/shard_map/project_q/pallas_call | solution.py:154
  88.8 0.0 collective-permute-done.3.refs_2_
  88.8 1.9 %collective-permute-start.12 = (bf16[1,256,128]{2,1,0:T(8,128)(2,1)S(1)}, bf16[1,256,128]{2,1,0:T(8,128)(2,1)S(1)}, u32[]{:S(2)}, u32[]{:S(2)}) collective-permute-start(bf16[1,256,128]{2,1,0:T(8,128)(2,1)S(1)} %slice.4), channel_id=1, source_target_pairs={{0,8},{8,16},{16,24},{24,32},{32,40},{40,48},{48,56},{56,64},{64,7... | collective-permute-start | bytes 196616 | tf_op jit(solution)/shard_map/ppermute | solution.py:368
  90.7 0.0 collective-permute-done.4.refs_3_
  90.7 0.0 copy-done.4
  90.7 0.0 copy-done.5
  90.7 0.0 copy-done.6
  90.7 0.0 copy-start.1
  90.8 0.9 copy-done.1
  91.7 4.1 %shard_map.91 = (f32[4,256,128]{2,1,0:T(8,128)S(1)}, f32[4,256,128]{2,1,0:T(8,128)S(1)}) custom-call(s32[2]{0:T(128)S(1)} %copy-done.5, bf16[4,256,128]{2,1,0:T(8,128)(2,1)S(1)} %copy-done.1, s32[256,1]{1,0:T(8,128)S(1)} %copy-done.4, bf16[1,256,128]{2,1,0:T(8,128)(2,1)S(1)} %bitcast.9, bf16[3,256,128]{2,1,0:T(8,128)(2,1)S(1)} %pad_maximum_fusion.1.refs_1_, ...), custom_call_target="tpu_custom_call" | custom-call | flops 536870912 | bytes 2097152 | tf_op jit(solution)/shard_map/pallas_call | solution.py:284
  95.8 0.0 collective-permute-done.7.refs_3_
  95.8 0.0 copy-start.2
  95.8 0.9 copy-done.2
  96.7 3.2 %shard_map.92 = (f32[4,256,128]{2,1,0:T(8,128)S(1)}, f32[4,256,128]{2,1,0:T(8,128)S(1)}) custom-call(s32[2]{0:T(128)S(1)} %copy-done.5, bf16[4,256,128]{2,1,0:T(8,128)(2,1)S(1)} %copy-done.2, s32[256,1]{1,0:T(8,128)S(1)} %copy-done.4, f32[4,256,128]{2,1,0:T(8,128)S(1)} %get-tuple-element.25.refs_0_, f32[4,256,128]{2,1,0:T(8,128)S(1)} %get-tuple-element.26.refs_1_, ...), custom_call_target="tpu_custom_call" | custom-call | flops 536870912 | bytes 2097152 | tf_op jit(solution)/shard_map/pallas_call | solution.py:284
  99.9 0.0 copy-start
  99.9 0.0 copy-start.3
  99.9 0.0 collective-permute-done.12.refs_0_
  99.9 2.1 %collective-permute-start.13 = (bf16[1,256,128]{2,1,0:T(8,128)(2,1)S(1)}, bf16[1,256,128]{2,1,0:T(8,128)(2,1)S(1)}, u32[]{:S(2)}, u32[]{:S(2)}) collective-permute-start(bf16[1,256,128]{2,1,0:T(8,128)(2,1)S(1)} %collective-permute-done.12.refs_0_), channel_id=1, source_target_pairs={{0,1},{1,0},{2,3},{3,2},{4,5},{5,4},{6,7},{7,6},{8,9},{9,8},{10,11... | collective-permute-start | bytes 196616 | tf_op jit(solution)/shard_map/ppermute | solution.py:372
  102.0 0.0 collective-permute-done.9.refs_3_
  102.0 2.7 %shard_map.93 = (f32[4,256,128]{2,1,0:T(8,128)S(1)}, f32[4,256,128]{2,1,0:T(8,128)S(1)}) custom-call(s32[2]{0:T(128)S(1)} %copy-done.5, bf16[4,256,128]{2,1,0:T(8,128)(2,1)S(1)} %copy-done.2, s32[256,1]{1,0:T(8,128)S(1)} %copy-done.4, f32[4,256,128]{2,1,0:T(8,128)S(1)} %get-tuple-element.27.refs_0_, f32[4,256,128]{2,1,0:T(8,128)S(1)} %get-tuple-element.28.refs_1_, ...), custom_call_target="tpu_custom_call" | custom-call | flops 536870912 | bytes 2097152 | tf_op jit(solution)/shard_map/pallas_call | solution.py:284
  104.7 0.0 collective-permute-done.11.refs_3_
  104.7 2.6 %shard_map.94 = (f32[4,256,128]{2,1,0:T(8,128)S(1)}, f32[4,256,128]{2,1,0:T(8,128)S(1)}) custom-call(s32[2]{0:T(128)S(1)} %copy-done.5, bf16[4,256,128]{2,1,0:T(8,128)(2,1)S(1)} %copy-done.2, s32[256,1]{1,0:T(8,128)S(1)} %copy-done.4, f32[4,256,128]{2,1,0:T(8,128)S(1)} %get-tuple-element.29.refs_0_, f32[4,256,128]{2,1,0:T(8,128)S(1)} %get-tuple-element.30.refs_1_, ...), custom_call_target="tpu_custom_call" | custom-call | flops 536870912 | bytes 2097152 | tf_op jit(solution)/shard_map/pallas_call | solution.py:284
  107.4 0.0 collective-permute-done.13.refs_1_
  107.4 0.0 copy-done
  107.4 0.0 copy-done.3
  107.4 1.9 %attend_far.1 = (bf16[4,256,256]{2,1,0:T(8,128)(2,1)S(1)}, bf16[4,256,256]{2,1,0:T(8,128)(2,1)S(1)}) custom-call(s32[2]{0:T(128)S(1)} %copy-done.5, bf16[4,256,128]{2,1,0:T(8,128)(2,1)S(1)} %copy-done.3, s32[256,1]{1,0:T(8,128)S(1)} %copy-done.4, f32[4,256,128]{2,1,0:T(8,128)S(1)} %get-tuple-element.31.total_in, ...), custom_call_target="tpu_custom_call" | custom-call | flops 134217728 | bytes 4194304 | tf_op jit(solution)/shard_map/attend_far/pallas_call | solution.py:342
  109.4 2.4 %collective-permute-start.14 = (bf16[4,256,256]{2,1,0:T(8,128)(2,1)S(1)}, bf16[4,256,256]{2,1,0:T(8,128)(2,1)S(1)}, u32[]{:S(2)}, u32[]{:S(2)}) collective-permute-start(bf16[4,256,256]{2,1,0:T(8,128)(2,1)S(1)} %get-tuple-element.34), channel_id=1, source_target_pairs={{0,1},{1,0},{2,3},{3,2},{4,5},{5,4},{6,7},{7,6},{8,9},{9,8},{10,11... | collective-permute-start | bytes 1572872 | tf_op jit(solution)/shard_map/ppermute | solution.py:372
  111.8 1.5 %collective-permute-done.14 = bf16[4,256,256]{2,1,0:T(8,128)(2,1)S(1)} collective-permute-done((bf16[4,256,256]{2,1,0:T(8,128)(2,1)S(1)}, bf16[4,256,256]{2,1,0:T(8,128)(2,1)S(1)}, u32[]{:S(2)}, u32[]{:S(2)}) %collective-permute-start.14) | collective-permute-done | bytes 524320 | tf_op jit(solution)/shard_map/ppermute | solution.py:372
  113.3 0.1 add_convert_fusion
  113.4 14.1 %all_to_all.5 = bf16[4,256,256]{2,1,0:T(8,128)(2,1)S(1)} all-to-all(bf16[4,256,256]{2,1,0:T(8,128)(2,1)S(1)} %add_convert_fusion), channel_id=1, replica_groups=mesh['ctx'=128,'x'=4,'c'=2] {'x'}, dimensions={0} | all-to-all | bytes 1048576 | tf_op jit(solution)/shard_map/all_to_all | solution.py:415
  127.5 0.7 reduce_sum.12
  (3 shorter events, 0.1 us)
Async XLA Ops:
  3.5 24.4 %collective-permute-start.1 = (bf16[256,128]{1,0:T(8,128)(2,1)}, bf16[256,128]{1,0:T(8,128)(2,1)S(1)}, u32[]{:S(2)}, u32[]{:S(2)}) collective-permute-start(bf16[256,128]{1,0:T(8,128)(2,1)} %get-tuple-element.24), channel_id=1, source_target_pairs={{0,40},{8,48},{16,56},{24,64},{32,72},{40,80},{48,88},{56,96},{64,... | collective-permute-start | bytes 196616 | tf_op jit(solution)/shard_map/ppermute | solution.py:368
  14.0 24.0 %collective-permute-start = (bf16[256,128]{1,0:T(8,128)(2,1)}, bf16[256,128]{1,0:T(8,128)(2,1)S(1)}, u32[]{:S(2)}, u32[]{:S(2)}) collective-permute-start(bf16[256,128]{1,0:T(8,128)(2,1)} %get-tuple-element.24), channel_id=1, source_target_pairs={{0,8},{8,16},{16,24},{24,32},{32,40},{40,48},{48,56},{56,64},{64,7... | collective-permute-start | bytes 196616 | tf_op jit(solution)/shard_map/ppermute | solution.py:368
  27.9 15.3 %collective-permute-start.2 = (bf16[256,128]{1,0:T(8,128)(2,1)S(1)}, bf16[256,128]{1,0:T(8,128)(2,1)S(1)}, u32[]{:S(2)}, u32[]{:S(2)}) collective-permute-start(bf16[256,128]{1,0:T(8,128)(2,1)S(1)} %collective-permute-done.1), channel_id=1, source_target_pairs={{0,32},{8,40},{16,48},{24,56},{32,64},{40,72},{48,80},{56,88},{64,... | collective-permute-start | bytes 196616 | tf_op jit(solution)/shard_map/ppermute | solution.py:368
  43.2 14.8 %collective-permute-start.5 = (bf16[3,256,128]{2,1,0:T(8,128)(2,1)S(1)}, bf16[3,256,128]{2,1,0:T(8,128)(2,1)S(1)}, u32[]{:S(2)}, u32[]{:S(2)}) collective-permute-start(bf16[3,256,128]{2,1,0:T(8,128)(2,1)S(1)} %pad_maximum_fusion.1.refs_1_), channel_id=1, source_target_pairs={{0,8},{8,16},{16,24},{24,32},{32,40},{40,48},{48,56},{56,64},{64,7... | collective-permute-start | bytes 589832 | tf_op jit(solution)/shard_map/ppermute | solution.py:368
  45.2 12.7 %collective-permute-start.6 = (bf16[256,128]{1,0:T(8,128)(2,1)S(1)}, bf16[256,128]{1,0:T(8,128)(2,1)S(1)}, u32[]{:S(2)}, u32[]{:S(2)}) collective-permute-start(bf16[256,128]{1,0:T(8,128)(2,1)S(1)} %collective-permute-done.2), channel_id=1, source_target_pairs={{0,32},{8,40},{16,48},{24,56},{32,64},{40,72},{48,80},{56,88},{64,... | collective-permute-start | bytes 196616 | tf_op jit(solution)/shard_map/ppermute | solution.py:368
  58.0 32.7 %copy-start.4 = (s32[256,1]{1,0:T(8,128)S(1)}, s32[256,1]{1,0:T(8,128)}, u32[]{:S(2)}) copy-start(s32[256,1]{1,0:T(8,128)} %get-tuple-element.23.starts) | copy-start | bytes 3076
  58.0 32.7 %copy-start.5 = (s32[2]{0:T(128)S(1)}, s32[2]{0:T(128)}, u32[]{:S(2)}) copy-start(s32[2]{0:T(128)} %get-tuple-element.20.span) | copy-start | bytes 28
  58.0 32.8 %copy-start.6 = (bf16[256,128]{1,0:T(8,128)(2,1)S(1)}, bf16[256,128]{1,0:T(8,128)(2,1)}, u32[]{:S(2)}) copy-start(bf16[256,128]{1,0:T(8,128)(2,1)} %get-tuple-element.24) | copy-start | bytes 196612
  58.0 11.0 %collective-permute-start.8 = (bf16[4,256,128]{2,1,0:T(8,128)(2,1)S(1)}, bf16[4,256,128]{2,1,0:T(8,128)(2,1)}, u32[]{:S(2)}, u32[]{:S(2)}) collective-permute-start(bf16[4,256,128]{2,1,0:T(8,128)(2,1)S(1)} %pad_maximum_fusion.refs_2_), channel_id=1, source_target_pairs={{0,8},{8,16},{16,24},{24,32},{32,40},{40,48},{48,56},{56,64},{64,7... | collective-permute-start | bytes 786440 | tf_op jit(solution)/shard_map/ppermute | solution.py:368
  69.0 10.7 %collective-permute-start.10 = (bf16[4,256,128]{2,1,0:T(8,128)(2,1)}, bf16[4,256,128]{2,1,0:T(8,128)(2,1)S(1)}, u32[]{:S(2)}, u32[]{:S(2)}) collective-permute-start(bf16[4,256,128]{2,1,0:T(8,128)(2,1)} %collective-permute-done.8.refs_2_), channel_id=1, source_target_pairs={{0,8},{8,16},{16,24},{24,32},{32,40},{40,48},{48,56},{56,64},{64,7... | collective-permute-start | bytes 786440 | tf_op jit(solution)/shard_map/ppermute | solution.py:368
  70.9 24.8 %collective-permute-start.7 = (bf16[4,256,128]{2,1,0:T(8,128)(2,1)S(1)}, bf16[4,256,128]{2,1,0:T(8,128)(2,1)}, u32[]{:S(2)}, u32[]{:S(2)}) collective-permute-start(bf16[4,256,128]{2,1,0:T(8,128)(2,1)S(1)} %pad_maximum_fusion.refs_2_), channel_id=1, source_target_pairs={{0,1},{1,0},{2,3},{3,2},{4,5},{5,4},{6,7},{7,6},{8,9},{9,8},{10,11... | collective-permute-start | bytes 786440 | tf_op jit(solution)/shard_map/ppermute | solution.py:372
  72.9 17.8 %collective-permute-start.4 = (bf16[3,256,128]{2,1,0:T(8,128)(2,1)S(1)}, bf16[3,256,128]{2,1,0:T(8,128)(2,1)}, u32[]{:S(2)}, u32[]{:S(2)}) collective-permute-start(bf16[3,256,128]{2,1,0:T(8,128)(2,1)S(1)} %pad_maximum_fusion.1.refs_1_), channel_id=1, source_target_pairs={{0,1},{1,0},{2,3},{3,2},{4,5},{5,4},{6,7},{7,6},{8,9},{9,8},{10,11... | collective-permute-start | bytes 589832 | tf_op jit(solution)/shard_map/ppermute | solution.py:372
  75.3 26.7 %collective-permute-start.9 = (bf16[4,256,128]{2,1,0:T(8,128)(2,1)}, bf16[4,256,128]{2,1,0:T(8,128)(2,1)}, u32[]{:S(2)}, u32[]{:S(2)}) collective-permute-start(bf16[4,256,128]{2,1,0:T(8,128)(2,1)} %collective-permute-done.8.refs_2_), channel_id=1, source_target_pairs={{0,1},{1,0},{2,3},{3,2},{4,5},{5,4},{6,7},{7,6},{8,9},{9,8},{10,11... | collective-permute-start | bytes 786440 | tf_op jit(solution)/shard_map/ppermute | solution.py:372
  79.7 25.0 %collective-permute-start.11 = (bf16[4,256,128]{2,1,0:T(8,128)(2,1)S(1)}, bf16[4,256,128]{2,1,0:T(8,128)(2,1)}, u32[]{:S(2)}, u32[]{:S(2)}) collective-permute-start(bf16[4,256,128]{2,1,0:T(8,128)(2,1)S(1)} %collective-permute-done.10.refs_2_), channel_id=1, source_target_pairs={{0,1},{1,0},{2,3},{3,2},{4,5},{5,4},{6,7},{7,6},{8,9},{9,8},{10,11... | collective-permute-start | bytes 786440 | tf_op jit(solution)/shard_map/ppermute | solution.py:372
  81.7 7.1 %collective-permute-start.3 = (bf16[1,256,128]{2,1,0:T(8,128)(2,1)}, bf16[1,256,128]{2,1,0:T(8,128)(2,1)}, u32[]{:S(2)}, u32[]{:S(2)}) collective-permute-start(bf16[1,256,128]{2,1,0:T(8,128)(2,1)} %bitcast.8), channel_id=1, source_target_pairs={{0,1},{1,0},{2,3},{3,2},{4,5},{5,4},{6,7},{7,6},{8,9},{9,8},{10,11... | collective-permute-start | bytes 196616 | tf_op jit(solution)/shard_map/ppermute | solution.py:372
  88.8 11.2 %collective-permute-start.12 = (bf16[1,256,128]{2,1,0:T(8,128)(2,1)S(1)}, bf16[1,256,128]{2,1,0:T(8,128)(2,1)S(1)}, u32[]{:S(2)}, u32[]{:S(2)}) collective-permute-start(bf16[1,256,128]{2,1,0:T(8,128)(2,1)S(1)} %slice.4), channel_id=1, source_target_pairs={{0,8},{8,16},{16,24},{24,32},{32,40},{40,48},{48,56},{56,64},{64,7... | collective-permute-start | bytes 196616 | tf_op jit(solution)/shard_map/ppermute | solution.py:368
  90.7 1.0 copy-start.1
  95.8 1.0 copy-start.2
  99.9 7.5 %copy-start = (bf16[512,2048]{1,0:T(8,128)(2,1)S(1)}, bf16[512,2048]{1,0:T(8,128)(2,1)}, u32[]{:S(2)}) copy-start(bf16[512,2048]{1,0:T(8,128)(2,1)} %refs_2_.1) | copy-start | bytes 6291460
  99.9 7.5 %copy-start.3 = (bf16[4,256,128]{2,1,0:T(8,128)(2,1)S(1)}, bf16[4,256,128]{2,1,0:T(8,128)(2,1)}, u32[]{:S(2)}) copy-start(bf16[4,256,128]{2,1,0:T(8,128)(2,1)} %project_q.1.queries) | copy-start | bytes 786436
  99.9 7.4 %collective-permute-start.13 = (bf16[1,256,128]{2,1,0:T(8,128)(2,1)S(1)}, bf16[1,256,128]{2,1,0:T(8,128)(2,1)S(1)}, u32[]{:S(2)}, u32[]{:S(2)}) collective-permute-start(bf16[1,256,128]{2,1,0:T(8,128)(2,1)S(1)} %collective-permute-done.12.refs_0_), channel_id=1, source_target_pairs={{0,1},{1,0},{2,3},{3,2},{4,5},{5,4},{6,7},{7,6},{8,9},{9,8},{10,11... | collective-permute-start | bytes 196616 | tf_op jit(solution)/shard_map/ppermute | solution.py:372
  109.4 3.9 %collective-permute-start.14 = (bf16[4,256,256]{2,1,0:T(8,128)(2,1)S(1)}, bf16[4,256,256]{2,1,0:T(8,128)(2,1)S(1)}, u32[]{:S(2)}, u32[]{:S(2)}) collective-permute-start(bf16[4,256,256]{2,1,0:T(8,128)(2,1)S(1)} %get-tuple-element.34), channel_id=1, source_target_pairs={{0,1},{1,0},{2,3},{3,2},{4,5},{5,4},{6,7},{7,6},{8,9},{9,8},{10,11... | collective-permute-start | bytes 1572872 | tf_op jit(solution)/shard_map/ppermute | solution.py:372
